TPU v7x, 32 devices: a whole 2x2x4 slice. The times are simulated.
32 devices in a mesh: wide: 8 (over z, y), narrow: 4 (over x, core).
Axes of the slice: x: 2, y: 2, z: 4, core: 2. Of those that a mesh axis runs over, the one named last changes fastest.
Arguments:
- inputs: bfloat16 [32, 192, 2048], P(('wide', 'narrow')), may hold values from -6 to 6
- counts: int32 [32], P(('wide', 'narrow')), may hold values from 0 to 48, as said below
- gain_attn: bfloat16 [2048], P(('wide', 'narrow')), may hold values from 0.5 to 1.5
- w_query: bfloat16 [2048, 2048], P(('wide', 'narrow')), may hold values from -0.125 to 0.125
- w_key: bfloat16 [2048, 2048], P(('wide', 'narrow')), may hold values from -0.125 to 0.125
- w_value: bfloat16 [2048, 2048], P(('wide', 'narrow')), may hold values from -0.125 to 0.125
- w_out: bfloat16 [2048, 2048], P(('wide', 'narrow')), may hold values from -0.5 to 0.5
- gain_mlp: bfloat16 [2048], P(('wide', 'narrow')), may hold values from 0.5 to 1.5
- w_up: bfloat16 [2048, 8192], P(('wide', 'narrow')), may hold values from -0.125 to 0.125
- w_down: bfloat16 [8192, 2048], P(('wide', 'narrow')), may hold values from -0.0625 to 0.0625
- cotangent: bfloat16 [32, 192, 2048], P(('wide', 'narrow')), may hold values from -6 to 6
Outputs:
- output: bfloat16 [32, 192, 2048], P(('wide', 'narrow'))
- grad_input: float32 [32, 192, 2048], P(('wide', 'narrow'))
- grad_gain_attn: float32 [2048], P(('wide', 'narrow'))
- grad_w_query: float32 [2048, 2048], P(('wide', 'narrow'))
- grad_w_key: float32 [2048, 2048], P(('wide', 'narrow'))
- grad_w_value: float32 [2048, 2048], P(('wide', 'narrow'))
- grad_w_out: float32 [2048, 2048], P(('wide', 'narrow'))
- grad_gain_mlp: float32 [2048], P(('wide', 'narrow'))
- grad_w_up: float32 [2048, 8192], P(('wide', 'narrow'))
- grad_w_down: float32 [8192, 2048], P(('wide', 'narrow'))
Inputs may be any that keep to these rules, and one draw needn't show every extreme that they name: Item i holds 144 image tokens followed by counts[i] text and action tokens; its slots from 144 + counts[i] to 191 are padding. Some item has 48 such tokens and some has none.
All inputs are finite; a program needn't handle non-finite values.
Results may differ from a plain program's by a relative error of at most 0.013.
Values may be sent and summed in bfloat16 or wider, within the bound.
No kernel may reach another device: no remote copies, remote signals or barrier semaphores. Data moves between devices by JAX's collectives and lax.ppermute only.
A program may use at most 512 MiB of HBM per device.

v0:
```python
import jax
import jax.numpy as jnp
from jax import lax
from jax.sharding import PartitionSpec as P

H = 16
HD = 128
IMAGE = 144


EPSILON = 1e-05
NEG_LARGE = -1e30


def matmul(left_side, right_side):
    return jnp.dot(left_side, right_side, preferred_element_type=jnp.float32)


def gram_rows(left_side, right_side):
    return lax.dot_general(
        left_side, right_side, (((0,), (0,)), ((), ())), preferred_element_type=jnp.float32
    )


def times_transposed(left_side, right_side):
    return lax.dot_general(
        left_side, right_side, (((1,), (1,)), ((), ())), preferred_element_type=jnp.float32
    )


def gelu_tanh(values):
    return jax.nn.gelu(values, approximate=True)


def norm_stats(values):
    center = values - jnp.mean(values, axis=-1, keepdims=True)
    inverse = lax.rsqrt(jnp.mean(center * center, axis=-1, keepdims=True) + EPSILON)
    return (center * inverse, inverse)


def norm_backward(grad_scaled, scaled, inverse):
    first_mean = jnp.mean(grad_scaled, axis=-1, keepdims=True)
    second_mean = jnp.mean(grad_scaled * scaled, axis=-1, keepdims=True)
    return inverse * (grad_scaled - first_mean - scaled * second_mean)


def masked_scores(queries, key_rows, allowed, score_scale):
    raw = jnp.einsum("ishd,ithd->ihst", queries, key_rows, preferred_element_type=jnp.float32)
    return jnp.where(allowed, raw * score_scale, NEG_LARGE)


def fetch_attn(gain_attn, w_query, w_key, w_value, w_out):
    return (
        lax.all_gather(gain_attn, ("wide", "narrow"), axis=0, tiled=True),
        lax.all_gather(w_query, ("wide", "narrow"), axis=0, tiled=True),
        lax.all_gather(w_key, ("wide", "narrow"), axis=0, tiled=True),
        lax.all_gather(w_value, ("wide", "narrow"), axis=0, tiled=True),
        lax.all_gather(w_out, ("wide", "narrow"), axis=0, tiled=True),
    )


def fetch_mlp(gain_mlp, w_up, w_down):
    return (
        lax.all_gather(gain_mlp, ("wide", "narrow"), axis=0, tiled=True),
        lax.all_gather(w_up, ("wide", "narrow"), axis=0, tiled=True),
        lax.all_gather(w_down, ("wide", "narrow"), axis=0, tiled=True),
    )


def per_device(
    inputs, counts, gain_attn, w_query, w_key, w_value, w_out, gain_mlp, w_up, w_down, cotangent
):
    item_count, slot_count, feature_count = inputs.shape
    row_count = item_count * slot_count
    score_scale = HD ** (-0.5)
    lengths = counts + IMAGE
    position = jnp.arange(slot_count)
    causal = (position[None, :] <= position[:, None])[None, None]
    allowed = causal & (position[None, None, None, :] < lengths[:, None, None, None])
    valid_rows = (position[None, :] < lengths[:, None]).astype(jnp.float32).reshape(row_count, 1)
    head_shape = (item_count, slot_count, H, HD)
    stream = inputs.reshape(row_count, feature_count).astype(jnp.float32)
    scaled_a, inverse_a = norm_stats(stream)
    attn_set = fetch_attn(gain_attn, w_query, w_key, w_value, w_out)
    normed_a_low = (scaled_a * attn_set[0].astype(jnp.float32)).astype(jnp.bfloat16)
    queries = matmul(normed_a_low, attn_set[1]).astype(jnp.bfloat16)
    key_rows = matmul(normed_a_low, attn_set[2]).astype(jnp.bfloat16)
    value_rows = matmul(normed_a_low, attn_set[3]).astype(jnp.bfloat16)
    queries = queries.reshape(head_shape)
    key_rows = key_rows.reshape(head_shape)
    value_rows = value_rows.reshape(head_shape)
    masked = masked_scores(queries, key_rows, allowed, score_scale)
    row_peak = jnp.max(masked, axis=-1, keepdims=True)
    shifted = jnp.exp(masked - row_peak)
    row_total = jnp.sum(shifted, axis=-1, keepdims=True)
    log_total = row_peak + jnp.log(row_total)
    probs_low = (shifted / row_total).astype(jnp.bfloat16)
    mixed_low = jnp.einsum(
        "ihst,ithd->ishd", probs_low, value_rows, preferred_element_type=jnp.float32
    )
    mixed_low = mixed_low.astype(jnp.bfloat16).reshape(row_count, feature_count)
    residual = stream + matmul(mixed_low, attn_set[4])
    scaled_m, inverse_m = norm_stats(residual)
    mlp_set = fetch_mlp(gain_mlp, w_up, w_down)
    normed_m_low = (scaled_m * mlp_set[0].astype(jnp.float32)).astype(jnp.bfloat16)
    hidden = matmul(normed_m_low, mlp_set[1])
    active_low = gelu_tanh(hidden).astype(jnp.bfloat16)
    output = residual + matmul(active_low, mlp_set[2])
    grad_stream = cotangent.reshape(row_count, feature_count).astype(jnp.float32) * valid_rows
    grad_low = grad_stream.astype(jnp.bfloat16)
    back_gain_m, back_up, back_down = fetch_mlp(gain_mlp, w_up, w_down)
    gelu_value, gelu_back = jax.vjp(gelu_tanh, hidden)
    grad_down = gram_rows(active_low, grad_low)
    grad_active = times_transposed(grad_low, back_down)
    grad_hidden = gelu_back(grad_active)[0].astype(jnp.bfloat16)
    grad_up = gram_rows(normed_m_low, grad_hidden)
    grad_normed_m = times_transposed(grad_hidden, back_up)
    grad_gain_m = jnp.sum(grad_normed_m * scaled_m, axis=0)
    grad_scaled_m = grad_normed_m * back_gain_m.astype(jnp.float32)
    gain_m_share, up_share, down_share = (
        lax.psum_scatter(grad_gain_m, ("wide", "narrow"), scatter_dimension=0, tiled=True),
        lax.psum_scatter(grad_up, ("wide", "narrow"), scatter_dimension=0, tiled=True),
        lax.psum_scatter(grad_down, ("wide", "narrow"), scatter_dimension=0, tiled=True),
    )
    grad_residual = norm_backward(grad_scaled_m, scaled_m, inverse_m) + grad_stream
    grad_residual_low = grad_residual.astype(jnp.bfloat16)
    back_gain_a, back_query, back_key, back_value, back_out = fetch_attn(
        gain_attn, w_query, w_key, w_value, w_out
    )
    grad_out_w = gram_rows(mixed_low, grad_residual_low)
    grad_mixed = times_transposed(grad_residual_low, back_out)
    grad_mixed = grad_mixed.astype(jnp.bfloat16).reshape(head_shape)
    masked_again = masked_scores(queries, key_rows, allowed, score_scale)
    attn_probs = jnp.exp(masked_again - log_total)
    probs_again = attn_probs.astype(jnp.bfloat16)
    grad_values = jnp.einsum(
        "ihst,ishd->ithd", probs_again, grad_mixed, preferred_element_type=jnp.float32
    ).astype(jnp.bfloat16)
    grad_probs = jnp.einsum(
        "ishd,ithd->ihst", grad_mixed, value_rows, preferred_element_type=jnp.float32
    )
    row_delta = jnp.sum(attn_probs * grad_probs, axis=-1, keepdims=True)
    grad_scores = (attn_probs * (grad_probs - row_delta)).astype(jnp.bfloat16)
    grad_queries = (
        jnp.einsum("ihst,ithd->ishd", grad_scores, key_rows, preferred_element_type=jnp.float32)
        * score_scale
    ).astype(jnp.bfloat16)
    grad_keys = (
        jnp.einsum("ihst,ishd->ithd", grad_scores, queries, preferred_element_type=jnp.float32)
        * score_scale
    ).astype(jnp.bfloat16)
    grad_queries = grad_queries.reshape(row_count, feature_count)
    grad_keys = grad_keys.reshape(row_count, feature_count)
    grad_values = grad_values.reshape(row_count, feature_count)
    grad_query_w = gram_rows(normed_a_low, grad_queries)
    grad_key_w = gram_rows(normed_a_low, grad_keys)
    grad_value_w = gram_rows(normed_a_low, grad_values)
    grad_normed_a = (
        times_transposed(grad_queries, back_query)
        + times_transposed(grad_keys, back_key)
        + times_transposed(grad_values, back_value)
    )
    grad_gain_a = jnp.sum(grad_normed_a * scaled_a, axis=0)
    grad_scaled_a = grad_normed_a * back_gain_a.astype(jnp.float32)
    shares = (
        lax.psum_scatter(grad_gain_a, ("wide", "narrow"), scatter_dimension=0, tiled=True),
        lax.psum_scatter(grad_query_w, ("wide", "narrow"), scatter_dimension=0, tiled=True),
        lax.psum_scatter(grad_key_w, ("wide", "narrow"), scatter_dimension=0, tiled=True),
        lax.psum_scatter(grad_value_w, ("wide", "narrow"), scatter_dimension=0, tiled=True),
        lax.psum_scatter(grad_out_w, ("wide", "narrow"), scatter_dimension=0, tiled=True),
    )
    grad_input = (norm_backward(grad_scaled_a, scaled_a, inverse_a) + grad_residual).reshape(
        item_count, slot_count, feature_count
    )
    return (
        output.reshape(item_count, slot_count, feature_count).astype(jnp.bfloat16),
        grad_input,
        shares[0],
        shares[1],
        shares[2],
        shares[3],
        shares[4],
        gain_m_share,
        up_share,
        down_share,
    )


def solution(mesh):
    return jax.shard_map(
        per_device,
        mesh=mesh,
        in_specs=(
            P(("wide", "narrow"), None, None),
            P(("wide", "narrow")),
            P(("wide", "narrow")),
            P(("wide", "narrow"), None),
            P(("wide", "narrow"), None),
            P(("wide", "narrow"), None),
            P(("wide", "narrow"), None),
            P(("wide", "narrow")),
            P(("wide", "narrow"), None),
            P(("wide", "narrow"), None),
            P(("wide", "narrow"), None, None),
        ),
        out_specs=(
            P(("wide", "narrow"), None, None),
            P(("wide", "narrow"), None, None),
            P(("wide", "narrow")),
            P(("wide", "narrow"), None),
            P(("wide", "narrow"), None),
            P(("wide", "narrow"), None),
            P(("wide", "narrow"), None),
            P(("wide", "narrow")),
            P(("wide", "narrow"), None),
            P(("wide", "narrow"), None),
        ),
        check_vma=False,
    )
```

profile of v0, /device:TPU:0, one launch (start us, length us, event | category | flops | bytes accessed | tf_op | source)
XLA Modules:
  0.0 2943.0 jit_solution(7602651469496119593)
XLA Ops:
  12.4 42.8 %all-reduce.5 = (bf16[2048]{0:T(1024)(128)(2,1)S(1)}, bf16[2048]{0:T(1024)(128)(2,1)S(1)}) all-reduce(bf16[2048]{0:T(1024)(128)(2,1)S(1)} %dynamic-update-slice, bf16[2048]{0:T(1024)(128)(2,1)S(1)} %dynamic-update-slice.1), channel_id=1, replica_groups=mesh['wide'=8,'narrow'=4] {'wide','narrow'}, use_global_device_ids=true, to_apply=%add | all-reduce | flops 4096 | bytes 16384
  55.9 35.1 %all-gather.11.cloned.1.call-done = bf16[2048,2048]{1,0:T(8,128)(2,1)} async-done(((bf16[64,2048]{1,0:T(8,128)(2,1)}), bf16[2048,2048]{1,0:T(8,128)(2,1)}) %all-gather.11.cloned.1.call-update) | async-done | bytes 8388624 | tf_op jit(solution)/shard_map/all_gather | solution.py:56
  97.1 72.4 %all-gather.9.cloned.1.call-done = bf16[2048,2048]{1,0:T(8,128)(2,1)} async-done(((bf16[64,2048]{1,0:T(8,128)(2,1)}), bf16[2048,2048]{1,0:T(8,128)(2,1)}) %all-gather.9.cloned.1.call-update) | async-done | bytes 8388624 | tf_op jit(solution)/shard_map/all_gather | solution.py:55
  176.2 71.8 %all-gather.7.cloned.1.call-done = bf16[2048,2048]{1,0:T(8,128)(2,1)} async-done(((bf16[64,2048]{1,0:T(8,128)(2,1)}), bf16[2048,2048]{1,0:T(8,128)(2,1)}) %all-gather.7.cloned.1.call-update) | async-done | bytes 8388624 | tf_op jit(solution)/shard_map/all_gather | solution.py:57
  255.9 70.6 %all-gather.13.cloned.1.call-done = bf16[2048,2048]{1,0:T(8,128)(2,1)} async-done(((bf16[64,2048]{1,0:T(8,128)(2,1)}), bf16[2048,2048]{1,0:T(8,128)(2,1)}) %all-gather.13.cloned.1.call-update) | async-done | bytes 8388624 | tf_op jit(solution)/shard_map/all_gather | solution.py:58
  333.6 188.4 %all-gather.15.cloned.1.call-done = bf16[2048,8192]{1,0:T(8,128)(2,1)} async-done(((bf16[64,8192]{1,0:T(8,128)(2,1)}), bf16[2048,8192]{1,0:T(8,128)(2,1)}) %all-gather.15.cloned.1.call-update) | async-done | bytes 33554448 | tf_op jit(solution)/shard_map/all_gather | solution.py:65
  522.0 18.3 fusion.99
  540.3 176.8 %all-gather.17.cloned.1.call-done = bf16[8192,2048]{1,0:T(8,128)(2,1)} async-done(((bf16[256,2048]{1,0:T(8,128)(2,1)}), bf16[8192,2048]{1,0:T(8,128)(2,1)}) %all-gather.17.cloned.1.call-update) | async-done | bytes 33554448 | tf_op jit(solution)/shard_map/all_gather | solution.py:66
  717.1 20.6 fusion.6
  737.6 20.3 multiply_reduce_fusion.1
  762.0 8.1 fusion.60
  779.3 8.4 fusion.50
  793.6 8.3 fusion.53
  805.8 8.3 fusion.56
  815.3 26.9 fusion.90
  843.6 26.0 fusion.98
  869.6 6.8 fusion.58
  887.3 41.8 %all-reduce.4 = (f32[2048]{0:T(1024)S(1)}, f32[2048]{0:T(1024)S(1)}) all-reduce(f32[2048]{0:T(1024)S(1)} %get-tuple-element.12, f32[2048]{0:T(1024)S(1)} %get-tuple-element.10), channel_id=2, replica_groups=mesh['wide'=8,'narrow'=4] {'wide','narrow'}, use_global_device_ids=true, to_apply=%region_12.13.clone | all-reduce | flops 4096 | bytes 32768
  933.9 21.0 fusion.9
  954.9 185.3 %reduce-scatter.11.cloned.1.call-done = f32[64,2048]{1,0:T(8,128)} async-done(((f32[2048,2048]{1,0:T(8,128)}), f32[64,2048]{1,0:T(8,128)}) %reduce-scatter.11.cloned.1.call-update) | async-done | bytes 524304 | tf_op jit(solution)/shard_map/reduce_scatter | solution.py:169
  1140.3 187.5 %reduce-scatter.9.cloned.1.call-done = f32[64,2048]{1,0:T(8,128)} async-done(((f32[2048,2048]{1,0:T(8,128)}), f32[64,2048]{1,0:T(8,128)}) %reduce-scatter.9.cloned.1.call-update) | async-done | bytes 524304 | tf_op jit(solution)/shard_map/reduce_scatter | solution.py:168
  1327.8 187.4 %reduce-scatter.7.cloned.1.call-done = f32[64,2048]{1,0:T(8,128)} async-done(((f32[2048,2048]{1,0:T(8,128)}), f32[64,2048]{1,0:T(8,128)}) %reduce-scatter.7.cloned.1.call-update) | async-done | bytes 524304 | tf_op jit(solution)/shard_map/reduce_scatter | solution.py:167
  1515.1 707.3 %reduce-scatter.17.cloned.1.call-done = f32[256,2048]{1,0:T(8,128)} async-done(((f32[8192,2048]{1,0:T(8,128)}), f32[256,2048]{1,0:T(8,128)}) %reduce-scatter.17.cloned.1.call-update) | async-done | bytes 2097168 | tf_op jit(solution)/shard_map/reduce_scatter | solution.py:123
  2222.5 713.2 %reduce-scatter.15.cloned.1.call-done = f32[64,8192]{1,0:T(8,128)} async-done(((f32[2048,8192]{1,0:T(8,128)}), f32[64,8192]{1,0:T(8,128)}) %reduce-scatter.15.cloned.1.call-update) | async-done | bytes 2097168 | tf_op jit(solution)/shard_map/reduce_scatter | solution.py:122
  (113 shorter events, 73.9 us)
Async XLA Ops:
  7.2 4.7 copy-start.16
  7.2 5.0 copy-start.17
  7.2 48.0 %copy-start = (bf16[1,192,2048]{2,1,0:T(8,128)(2,1)S(1)}, bf16[1,192,2048]{2,1,0:T(8,128)(2,1)}, u32[]{:S(2)}) copy-start(bf16[1,192,2048]{2,1,0:T(8,128)(2,1)} %param.11) | copy-start | bytes 2359300
  7.2 83.7 %all-gather.11.cloned.1.call-start = ((), (), s32[]{:S(2)}) async-start(), calls=%async_computation.8 | async-start | bytes 8650752 | tf_op jit(solution)/shard_map/all_gather | solution.py:56
  7.9 161.6 %all-gather.9.cloned.1.call-start = ((), (), s32[]{:S(2)}) async-start(), calls=%async_computation.7 | async-start | bytes 8650752 | tf_op jit(solution)/shard_map/all_gather | solution.py:55
  8.7 239.4 %all-gather.7.cloned.1.call-start = ((), (), s32[]{:S(2)}) async-start(), calls=%async_computation.6 | async-start | bytes 8650752 | tf_op jit(solution)/shard_map/all_gather | solution.py:57
  9.4 317.1 %all-gather.13.cloned.1.call-start = ((), (), s32[]{:S(2)}) async-start(), calls=%async_computation.9 | async-start | bytes 8650752 | tf_op jit(solution)/shard_map/all_gather | solution.py:58
  10.0 512.0 %all-gather.15.cloned.1.call-start = ((), (), s32[]{:S(2)}) async-start(), calls=%async_computation.10 | async-start | bytes 34603008 | tf_op jit(solution)/shard_map/all_gather | solution.py:65
  10.6 706.5 %all-gather.17.cloned.1.call-start = ((), (), s32[]{:S(2)}) async-start(), calls=%async_computation.11 | async-start | bytes 34603008 | tf_op jit(solution)/shard_map/all_gather | solution.py:66
  11.2 943.8 %reduce-scatter.13.cloned.1.call-start = ((), (), s32[]{:S(2)}) async-start(), calls=%async_computation.15 | async-start | bytes 17301504 | tf_op jit(solution)/shard_map/reduce_scatter | solution.py:170
  169.5 5.3 copy-start.14
  757.9 4.1 copy-start.8
  770.1 370.2 %reduce-scatter.11.cloned.1.call-start = ((), (), s32[]{:S(2)}) async-start(), calls=%async_computation.14 | async-start | bytes 17301504 | tf_op jit(solution)/shard_map/reduce_scatter | solution.py:169
  777.9 1.4 copy-start.1
  787.7 540.0 %reduce-scatter.9.cloned.1.call-start = ((), (), s32[]{:S(2)}) async-start(), calls=%async_computation.13 | async-start | bytes 17301504 | tf_op jit(solution)/shard_map/reduce_scatter | solution.py:168
  802.0 1.4 copy-start.7
  802.0 713.2 %reduce-scatter.7.cloned.1.call-start = ((), (), s32[]{:S(2)}) async-start(), calls=%async_computation.12 | async-start | bytes 17301504 | tf_op jit(solution)/shard_map/reduce_scatter | solution.py:167
  805.8 8.3 copy-start.12
  814.2 1408.3 %reduce-scatter.17.cloned.1.call-start = ((), (), s32[]{:S(2)}) async-start(), calls=%async_computation.17 | async-start | bytes 69206016 | tf_op jit(solution)/shard_map/reduce_scatter | solution.py:123
  842.2 1.4 copy-start.4
  842.2 2093.5 %reduce-scatter.15.cloned.1.call-start = ((), (), s32[]{:S(2)}) async-start(), calls=%async_computation.16 | async-start | bytes 69206016 | tf_op jit(solution)/shard_map/reduce_scatter | solution.py:122
  869.6 13.3 slice-start
  876.4 6.6 copy-start.11
  876.4 6.6 slice-start.1
  (10 other events, 10.5 us)
Sparse Core Ops, SparseCore 0:
  10.9 80.0 all-gather.10
  93.8 75.6 all-gather.8
  172.4 75.6 all-gather.6
  250.8 75.6 all-gather.12
  329.2 192.7 all-gather.14
  524.7 192.3 all-gather.16
  770.2 182.4 reduce-scatter.12
  955.6 184.6 reduce-scatter.10
  1143.2 184.5 reduce-scatter.8
  1330.5 184.5 reduce-scatter.6
  1518.1 704.3 reduce-scatter.16
  2225.2 710.3 reduce-scatter.14
where the time goes:
time: 2960 us; the launch traced here: 2940 us
  waiting for transfers between devices  2600 us (88%)
  matrix products  220 us (7%)
  blocking collectives  84.5 us (3%)
    reduce_scatter x1, waiting for transfers between devices, per_device(): lax.psum_scatter(grad_up, ('wide', 'narrow'), scatter_dimension=0, tiled=...  713 us
    reduce_scatter x1, waiting for transfers between devices, per_device(): lax.psum_scatter(grad_down, ('wide', 'narrow'), scatter_dimension=0, tile...  707 us
    all_gather x1, waiting for transfers between devices, fetch_mlp(): lax.all_gather(w_up, ('wide', 'narrow'), axis=0, tiled=True)  188 us
    reduce_scatter x1, waiting for transfers between devices, per_device(): lax.psum_scatter(grad_key_w, ('wide', 'narrow'), scatter_dimension=0, til...  188 us
    reduce_scatter x1, waiting for transfers between devices, per_device(): lax.psum_scatter(grad_query_w, ('wide', 'narrow'), scatter_dimension=0, t...  187 us
    reduce_scatter x1, waiting for transfers between devices, per_device(): lax.psum_scatter(grad_value_w, ('wide', 'narrow'), scatter_dimension=0, t...  185 us
    all_gather x1, waiting for transfers between devices, fetch_mlp(): lax.all_gather(w_down, ('wide', 'narrow'), axis=0, tiled=True)  177 us
    dot_general x6, matrix products, gram_rows(): lax.dot_general(left_side, right_side, (((0,), (0,)), ((), ())), preferre...  86 us
  transfers between devices with their start and end apart: 12, of which 11 were waited for; matrix products, arithmetic and copies ran while one was open for 6% of the time, Pallas kernels for 0%

commit v1 on v0

v1 whole, which is shorter than its diff:
```python
import jax
import jax.numpy as jnp
from jax import lax
from jax.sharding import Mesh, PartitionSpec as P

H = 16
HD = 128
IMAGE = 144
EPSILON = 1e-05
NEG_LARGE = -1e30

ALL = ("z", "y", "x", "c")
TEAM = ("y", "x", "c")
SWAP = [(0, 1), (1, 0)]


def matmul(left_side, right_side):
    return jnp.dot(left_side, right_side, preferred_element_type=jnp.float32)


def gram_rows(left_side, right_side):
    return lax.dot_general(
        left_side, right_side, (((0,), (0,)), ((), ())), preferred_element_type=jnp.float32
    )


def times_transposed(left_side, right_side):
    return lax.dot_general(
        left_side, right_side, (((1,), (1,)), ((), ())), preferred_element_type=jnp.float32
    )


def gelu_tanh(values):
    return jax.nn.gelu(values, approximate=True)


def norm_stats(values):
    center = values - jnp.mean(values, axis=-1, keepdims=True)
    inverse = lax.rsqrt(jnp.mean(center * center, axis=-1, keepdims=True) + EPSILON)
    return (center * inverse, inverse)


def norm_backward(grad_scaled, scaled, inverse):
    first_mean = jnp.mean(grad_scaled, axis=-1, keepdims=True)
    second_mean = jnp.mean(grad_scaled * scaled, axis=-1, keepdims=True)
    return inverse * (grad_scaled - first_mean - scaled * second_mean)


def swap(block, axis):
    return lax.ppermute(block, axis, SWAP)


def team_gather(block):
    half = block.shape[0] // 2
    by_x = swap(block, "x")
    by_y = swap(block, "y")
    by_c = swap(block, "c")
    corner = jnp.concatenate([swap(by_x[:half], "y"), swap(by_y[half:], "x")], axis=0)
    return jnp.concatenate(
        [block, by_c, by_x, swap(by_x, "c"), by_y, swap(by_y, "c"), corner, swap(corner, "c")], axis=0
    )


def team_sum(parts):
    low = jnp.bfloat16
    half = parts.shape[1] // 2

    def pair(k):
        return parts[k].astype(jnp.float32) + swap(parts[k + 1], "c").astype(jnp.float32)

    corner = pair(6).astype(low)
    on_x = pair(2)
    on_y = pair(4)
    from_x = swap(corner[:half], "x").astype(jnp.float32)
    from_y = swap(corner[half:], "y").astype(jnp.float32)
    x_first = swap(on_x[:half].astype(low), "x")
    y_last = swap(on_y[half:].astype(low), "y")
    own = pair(0)
    y_first = swap((on_y[:half] + from_x).astype(low), "y")
    x_last = swap((on_x[half:] + from_y).astype(low), "x")
    return (
        own
        + jnp.concatenate([x_first, x_last], axis=0).astype(jnp.float32)
        + jnp.concatenate([y_first, y_last], axis=0).astype(jnp.float32)
    )


def weight_gather(block):
    return lax.all_gather(block, "z", axis=0, tiled=True)


def weight_scatter(terms):
    return lax.psum_scatter(terms.astype(jnp.bfloat16), "z", scatter_dimension=0, tiled=True)


def masked_scores(queries, key_rows, allowed, score_scale):
    raw = jnp.einsum("ishd,ithd->ihst", queries, key_rows, preferred_element_type=jnp.float32)
    return jnp.where(allowed, raw * score_scale, NEG_LARGE)


def per_device(
    inputs, counts, gain_attn, w_query, w_key, w_value, w_out, gain_mlp, w_up, w_down, cotangent
):
    low = jnp.bfloat16
    layers = lax.axis_size("z")
    team = lax.axis_size(TEAM)
    devices = layers * team
    item_count, slot_count, features = inputs.shape
    assert item_count == 1
    row_count = item_count * slot_count
    wide_rows = row_count * team
    depth = w_query.shape[0]
    head_parts = HD // depth
    head_axes = TEAM[len(TEAM) - (head_parts.bit_length() - 1) :]
    head_groups = team // head_parts
    own_heads = layers // head_parts
    own_width = own_heads * HD
    units = w_down.shape[0]
    own_units = layers * units
    score_scale = HD ** (-0.5)

    def own_columns(weight):
        cut = weight.reshape(depth, head_parts, own_heads, head_groups, HD)
        return cut.transpose(3, 1, 0, 2, 4).reshape(team, depth, own_width)

    qkv_cut = jnp.concatenate([own_columns(w_query), own_columns(w_key), own_columns(w_value)], axis=2)
    qkv_cut = lax.all_to_all(qkv_cut, TEAM, 0, 0, tiled=True)
    w_qkv = weight_gather(qkv_cut.reshape(team * depth, 3 * own_width))
    out_rows = weight_gather(w_out)

    small = jnp.stack(
        [gain_attn, gain_mlp, jnp.broadcast_to(counts.astype(low)[:1], gain_attn.shape)], axis=0
    )
    small = lax.all_to_all(
        jnp.broadcast_to(small[None], (devices,) + small.shape), ALL, 0, 0, tiled=True
    )
    full_gain_a = small[:, 0].reshape(1, features).astype(jnp.float32)
    full_gain_m = small[:, 1].reshape(1, features).astype(jnp.float32)
    member = lax.axis_index("z") * team + (lax.axis_index(TEAM) ^ jnp.arange(team))
    picked = member[:, None] == jnp.arange(devices)[None, :]
    team_counts = jnp.sum(jnp.where(picked, small[:, 2, 0].astype(jnp.float32)[None, :], 0.0), axis=1)

    stream = inputs.reshape(row_count, features).astype(jnp.float32)
    scaled_a, inverse_a = norm_stats(stream)
    normed_a = team_gather((scaled_a * full_gain_a).astype(low))

    up_cut = w_up.reshape(depth, layers, team, units).transpose(2, 0, 1, 3)
    up_cut = lax.all_to_all(up_cut.reshape(team, depth, own_units), TEAM, 0, 0, tiled=True)
    w_up_own = weight_gather(up_cut.reshape(team * depth, own_units))
    w_down_own = weight_gather(w_down)

    position = jnp.arange(slot_count)
    lengths = counts + IMAGE
    live = (position[None, :] < lengths[:, None]).reshape(row_count, 1)
    cotangent_low = jnp.where(live, cotangent.reshape(row_count, features), jnp.zeros((), low))
    grad_stream = cotangent_low.astype(jnp.float32)
    grad_low = team_gather(cotangent_low)

    out_cut = out_rows.reshape(head_parts, own_heads, depth, features)
    out_cut = lax.all_to_all(out_cut, head_axes, 0, 0, tiled=True)
    w_out_own = out_cut.transpose(1, 0, 2, 3).reshape(own_width, features)

    qkv = matmul(normed_a, w_qkv).astype(low)
    head_shape = (team, slot_count, own_heads, HD)
    queries = qkv[:, :own_width].reshape(head_shape)
    key_rows = qkv[:, own_width : 2 * own_width].reshape(head_shape)
    value_rows = qkv[:, 2 * own_width :].reshape(head_shape)
    causal = (position[None, :] <= position[:, None])[None, None]
    live_keys = position[None, :].astype(jnp.float32) < team_counts[:, None] + float(IMAGE)
    allowed = causal & live_keys[:, None, None, :]
    masked = masked_scores(queries, key_rows, allowed, score_scale)
    row_peak = jnp.max(masked, axis=-1, keepdims=True)
    shifted = jnp.exp(masked - row_peak)
    attn_probs = shifted / jnp.sum(shifted, axis=-1, keepdims=True)
    probs_low = attn_probs.astype(low)
    mixed = jnp.einsum("ihst,ithd->ishd", probs_low, value_rows, preferred_element_type=jnp.float32)
    mixed = mixed.astype(low).reshape(wide_rows, own_width)
    out_terms = matmul(mixed, w_out_own).astype(low)
    residual = stream + team_sum(out_terms.reshape(team, row_count, features))

    scaled_m, inverse_m = norm_stats(residual)
    normed_m = team_gather((scaled_m * full_gain_m).astype(low))
    hidden = matmul(normed_m, w_up_own)
    gelu_value, gelu_back = jax.vjp(gelu_tanh, hidden)
    active = gelu_value.astype(low)
    down_terms = matmul(active, w_down_own).astype(low)
    output = residual + team_sum(down_terms.reshape(team, row_count, features))

    grad_active = times_transposed(grad_low, w_down_own)
    grad_hidden = gelu_back(grad_active)[0].astype(low)
    normed_m_terms = times_transposed(grad_hidden, w_up_own).astype(low)
    grad_normed_m = team_sum(normed_m_terms.reshape(team, row_count, features))
    grad_down = weight_scatter(gram_rows(active, grad_low))
    grad_up = weight_scatter(gram_rows(normed_m, grad_hidden))
    gain_m_terms = jnp.sum(grad_normed_m * scaled_m, axis=0)
    grad_residual = norm_backward(grad_normed_m * full_gain_m, scaled_m, inverse_m) + grad_stream

    grad_residual_low = team_gather(grad_residual.astype(low))
    grad_out = gram_rows(mixed, grad_residual_low).astype(low)
    grad_out = grad_out.reshape(own_heads, head_parts, depth, features).transpose(1, 0, 2, 3)
    grad_out = lax.all_to_all(grad_out, head_axes, 0, 0, tiled=True)
    grad_out = weight_scatter(grad_out.reshape(layers * depth, features))
    grad_mixed = times_transposed(grad_residual_low, w_out_own).astype(low).reshape(head_shape)
    grad_values = jnp.einsum(
        "ihst,ishd->ithd", probs_low, grad_mixed, preferred_element_type=jnp.float32
    ).astype(low)
    grad_probs = jnp.einsum(
        "ishd,ithd->ihst", grad_mixed, value_rows, preferred_element_type=jnp.float32
    )
    row_delta = jnp.sum(attn_probs * grad_probs, axis=-1, keepdims=True)
    grad_scores = (attn_probs * (grad_probs - row_delta)).astype(low)
    grad_queries = (
        jnp.einsum("ihst,ithd->ishd", grad_scores, key_rows, preferred_element_type=jnp.float32)
        * score_scale
    ).astype(low)
    grad_keys = (
        jnp.einsum("ihst,ishd->ithd", grad_scores, queries, preferred_element_type=jnp.float32)
        * score_scale
    ).astype(low)
    grad_qkv = jnp.concatenate(
        [part.reshape(wide_rows, own_width) for part in (grad_queries, grad_keys, grad_values)], axis=1
    )
    normed_a_terms = times_transposed(grad_qkv, w_qkv).astype(low)
    grad_qkv_w = weight_scatter(gram_rows(normed_a, grad_qkv))
    grad_normed_a = team_sum(normed_a_terms.reshape(team, row_count, features))
    gain_a_terms = jnp.sum(grad_normed_a * scaled_a, axis=0)
    grad_input = norm_backward(grad_normed_a * full_gain_a, scaled_a, inverse_a) + grad_residual

    gain_terms = jnp.stack([gain_a_terms, gain_m_terms], axis=0).reshape(2, devices, depth)
    gain_terms = lax.all_to_all(gain_terms.transpose(1, 0, 2), ALL, 0, 0, tiled=True)
    gain_grads = jnp.sum(gain_terms, axis=0)

    def all_columns(cut):
        cut = cut.reshape(head_groups, head_parts, depth, own_heads, HD)
        return cut.transpose(2, 1, 3, 0, 4).reshape(depth, features).astype(jnp.float32)

    grad_up = lax.all_to_all(grad_up.reshape(team, depth, own_units), TEAM, 0, 0, tiled=True)
    grad_up = grad_up.reshape(team, depth, layers, units).transpose(1, 2, 0, 3)
    grad_up = grad_up.reshape(depth, layers * team * units).astype(jnp.float32)
    back = lax.all_to_all(grad_qkv_w.reshape(team, depth, 3 * own_width), TEAM, 0, 0, tiled=True)

    return (
        output.reshape(item_count, slot_count, features).astype(low),
        grad_input.reshape(item_count, slot_count, features),
        gain_grads[0],
        all_columns(back[:, :, :own_width]),
        all_columns(back[:, :, own_width : 2 * own_width]),
        all_columns(back[:, :, 2 * own_width :]),
        grad_out.astype(jnp.float32),
        gain_grads[1],
        grad_up,
        grad_down.astype(jnp.float32),
    )


def solution(mesh):
    wide, narrow = mesh.shape["wide"], mesh.shape["narrow"]
    steps = Mesh(mesh.devices.reshape(wide // 2, 2, narrow // 2, 2), ALL)
    rows, items = P(ALL, None), P(ALL, None, None)
    return jax.shard_map(
        per_device,
        mesh=steps,
        in_specs=(items, P(ALL), P(ALL), rows, rows, rows, rows, P(ALL), rows, rows, items),
        out_specs=(items, items, P(ALL), rows, rows, rows, rows, P(ALL), rows, rows),
        check_vma=False,
    )
```

time: 2960 us -> 672 us (0.23)
  waiting for transfers between devices: 2600 us -> 315 us
  matrix products: 220 us -> 110 us
  starting transfers between devices: 0.86 us -> 67.8 us
  local copies, waits for them, and re-layouts: 13.4 us -> 75.7 us
  blocking collectives: 84.5 us -> 38.6 us
  other arithmetic: 8.79 us -> 41.3 us
    reduce_scatter x6 -> x4, waiting for transfers between devices: 1980 us -> 85.3 us  [weight_scatter(): lax.psum_scatter(terms.astype(jnp.bfloat16), 'z', scatter_dimension=0, ti...]
    all_gather x6 -> x4, waiting for transfers between devices: 615 us -> 21.2 us  [weight_gather(): return lax.all_gather(block, 'z', axis=0, tiled=True)]
    ppermute x0 -> x72, waiting for transfers between devices: none -> 192 us  [swap(): return lax.ppermute(block, axis, SWAP)]
    unnamed x2 -> x0, blocking collectives: 84.5 us -> none
    ppermute x0 -> x72, starting transfers between devices: none -> 51 us  [swap(): return lax.ppermute(block, axis, SWAP)]
    dot_general x6 -> x4, matrix products: 86 us -> 38.2 us  [gram_rows(): lax.dot_general(left_side, right_side, (((0,), (0,)), ((), ())), preferre...]
    all_to_all x0 -> x4, blocking collectives: none -> 38.6 us  [the longest x1 17.8 us: per_device(): qkv_cut = lax.all_to_all(qkv_cut, TEAM, 0, 0, tiled=True)]
    dot_general x6 -> x4, matrix products: 65.2 us -> 33.4 us  [times_transposed(): lax.dot_general(left_side, right_side, (((1,), (1,)), ((), ())), preferre...]
  transfers between devices with their start and end apart: 12 -> 84, of which waited for: 11 -> 38; matrix products, arithmetic and copies ran while one was open for 6% -> 28% of each run, Pallas kernels for 0% -> 0%
where the time goes in v1:
time: 672 us; the launch traced here: 665 us
  waiting for transfers between devices  315 us (47%)
  matrix products  110 us (16%)
  local copies, waits for them, and re-layouts  75.7 us (11%)
  starting transfers between devices  67.8 us (10%)
  other arithmetic  41.3 us (6%)
  blocking collectives  38.6 us (6%)
  between operations  16.2 us (2%)
    ppermute x72, waiting for transfers between devices, swap(): return lax.ppermute(block, axis, SWAP)  192 us
    reduce_scatter x4, waiting for transfers between devices, weight_scatter(): lax.psum_scatter(terms.astype(jnp.bfloat16), 'z', scatter_dimension=0, ti...  85.3 us
    ppermute x72, starting transfers between devices, swap(): return lax.ppermute(block, axis, SWAP)  51 us
    dot_general x4, matrix products, gram_rows(): lax.dot_general(left_side, right_side, (((0,), (0,)), ((), ())), preferre...  38.2 us
    unnamed x106, local copies, waits for them, and re-layouts  37.2 us
    dot_general x4, matrix products, times_transposed(): lax.dot_general(left_side, right_side, (((1,), (1,)), ((), ())), preferre...  33.4 us
    dot_general x4, matrix products, matmul(): return jnp.dot(left_side, right_side, preferred_element_type=jnp.float32)  32.8 us
    all_gather x4, waiting for transfers between devices, weight_gather(): return lax.all_gather(block, 'z', axis=0, tiled=True)  21.2 us
  transfers between devices with their start and end apart: 84, of which 38 were waited for; matrix products, arithmetic and copies ran while one was open for 28% of the time, Pallas kernels for 0%

profile of v1, /device:TPU:0, one launch (start us, length us, event | category | flops | bytes accessed | tf_op | source)
XLA Modules:
  0.0 665.5 jit_solution(13346239546717310166)
XLA Ops:
  11.7 17.8 %all_to_all.40 = bf16[8,64,768]{2,1,0:T(8,128)(2,1)} all-to-all(bf16[8,64,768]{2,1,0:T(8,128)(2,1)S(1)} %pad_maximum_fusion.1), channel_id=1, replica_groups=mesh['z'=4,'y'=2,'x'=2,'c'=2] {'y','x','c'}, dimensions={0} | all-to-all | bytes 1572864 | tf_op jit(solution)/shard_map/all_to_all | solution.py:127
  51.5 25.9 %collective-permute-done.1 = bf16[192,2048]{1,0:T(8,128)(2,1)S(1)} collective-permute-done((bf16[192,2048]{1,0:T(8,128)(2,1)S(1)}, bf16[192,2048]{1,0:T(8,128)(2,1)S(1)}, u32[]{:S(2)}, u32[]{:S(2)}) %collective-permute-start.1) | collective-permute-done | bytes 786464 | tf_op jit(solution)/shard_map/ppermute | solution.py:50
  117.6 8.1 %convolution_convert_fusion.6 = bf16[1536,768]{1,0:T(8,128)(2,1)S(1)} fusion(bf16[1536,2048]{1,0:T(8,128)(2,1)} %constant_dynamic-update-slice_fusion, bf16[2048,768]{1,0:T(8,128)(2,1)} %all-gather.5.cloned.1.call-done), kind=kOutput, calls=%fused_computation.17 | convolution fusion | flops 4833017856 | bytes 11796480 | tf_op jit(solution)/shard_map/dot_general | solution.py:18
  154.2 12.5 %collective-permute-done.12 = bf16[96,2048]{1,0:T(8,128)(2,1)S(1)} collective-permute-done((bf16[96,2048]{1,0:T(8,128)(2,1)S(1)}, bf16[96,2048]{1,0:T(8,128)(2,1)S(1)}, u32[]{:S(2)}, u32[]{:S(2)}) %collective-permute-start.12) | collective-permute-done | bytes 393248 | tf_op jit(solution)/shard_map/ppermute | solution.py:50
  168.3 8.6 %collective-permute-done.15 = bf16[96,2048]{1,0:T(8,128)(2,1)S(1)} collective-permute-done((bf16[96,2048]{1,0:T(8,128)(2,1)S(1)}, bf16[96,2048]{1,0:T(8,128)(2,1)S(1)}, u32[]{:S(2)}, u32[]{:S(2)}) %collective-permute-start.15) | collective-permute-done | bytes 393248 | tf_op jit(solution)/shard_map/ppermute | solution.py:50
  181.3 7.5 %collective-permute-done.17 = bf16[96,2048]{1,0:T(8,128)(2,1)S(1)} collective-permute-done((bf16[96,2048]{1,0:T(8,128)(2,1)S(1)}, bf16[96,2048]{1,0:T(8,128)(2,1)S(1)}, u32[]{:S(2)}, u32[]{:S(2)}) %collective-permute-start.17) | collective-permute-done | bytes 393248 | tf_op jit(solution)/shard_map/ppermute | solution.py:50
  202.7 13.3 %collective-permute-done.19 = bf16[192,2048]{1,0:T(8,128)(2,1)S(1)} collective-permute-done((bf16[192,2048]{1,0:T(8,128)(2,1)S(1)}, bf16[192,2048]{1,0:T(8,128)(2,1)S(1)}, u32[]{:S(2)}, u32[]{:S(2)}) %collective-permute-start.19) | collective-permute-done | bytes 786464 | tf_op jit(solution)/shard_map/ppermute | solution.py:50
  234.6 11.8 %fusion.75 = f32[1536,1024]{1,0:T(8,128)} fusion(bf16[1536,2048]{1,0:T(8,128)(2,1)} %constant_dynamic-update-slice_fusion.9, bf16[2048,1024]{1,0:T(8,128)(2,1)} %all-gather.9.cloned.1.call-done), kind=kOutput, calls=%fused_computation.216 | convolution fusion | flops 6442450944 | bytes 16777216 | tf_op jit(solution)/shard_map/dot_general | solution.py:18
  246.4 21.2 %all-gather.11.cloned.1.call-done = bf16[1024,2048]{1,0:T(8,128)(2,1)} async-done(((bf16[256,2048]{1,0:T(8,128)(2,1)}), bf16[1024,2048]{1,0:T(8,128)(2,1)}) %all-gather.11.cloned.1.call-update) | async-done | bytes 4194320 | tf_op jit(solution)/shard_map/all_gather | solution.py:89
  267.6 14.3 %fusion.7 = bf16[1536,1024]{1,0:T(8,128)(2,1)S(1)} fusion(f32[1536,1024]{1,0:T(8,128)} %fusion.75, bf16[1536,2048]{1,0:T(8,128)(2,1)} %copy-done.23, bf16[1024,2048]{1,0:T(8,128)(2,1)} %all-gather.11.cloned.1.call-done), kind=kOutput, calls=%fused_computation.13 | convolution fusion | flops 6473908224 | bytes 19922944 | tf_op jit(solution)/shard_map/dot_general | solution.py:28
  292.9 11.1 %convolution_convert_fusion.3 = bf16[1536,2048]{1,0:T(8,128)(2,1)S(1)} fusion(bf16[1024,2048]{1,0:T(8,128)(2,1)S(1)} %copy-done.31, f32[1536,1024]{1,0:T(8,128)} %fusion.75), kind=kOutput, calls=%fused_computation.6 | convolution fusion | flops 6459752448 | bytes 16777216 | tf_op jit(solution)/shard_map/dot_general | solution.py:18
  311.9 14.5 %collective-permute-done.48 = bf16[96,2048]{1,0:T(8,128)(2,1)S(1)} collective-permute-done((bf16[96,2048]{1,0:T(8,128)(2,1)S(1)}, bf16[96,2048]{1,0:T(8,128)(2,1)S(1)}, u32[]{:S(2)}, u32[]{:S(2)}) %collective-permute-start.48) | collective-permute-done | bytes 393248 | tf_op jit(solution)/shard_map/ppermute | solution.py:50
  328.0 8.7 %collective-permute-done.51 = bf16[96,2048]{1,0:T(8,128)(2,1)S(1)} collective-permute-done((bf16[96,2048]{1,0:T(8,128)(2,1)S(1)}, bf16[96,2048]{1,0:T(8,128)(2,1)S(1)}, u32[]{:S(2)}, u32[]{:S(2)}) %collective-permute-start.51) | collective-permute-done | bytes 393248 | tf_op jit(solution)/shard_map/ppermute | solution.py:50
  338.3 7.9 %collective-permute-done.33 = bf16[96,2048]{1,0:T(8,128)(2,1)S(1)} collective-permute-done((bf16[96,2048]{1,0:T(8,128)(2,1)S(1)}, bf16[96,2048]{1,0:T(8,128)(2,1)S(1)}, u32[]{:S(2)}, u32[]{:S(2)}) %collective-permute-start.33) | collective-permute-done | bytes 393248 | tf_op jit(solution)/shard_map/ppermute | solution.py:50
  388.6 11.2 %convolution_convert_fusion.5 = bf16[2048,1024]{1,0:T(8,128)(2,1)} fusion(bf16[1536,2048]{1,0:T(8,128)(2,1)} %constant_dynamic-update-slice_fusion.9, bf16[1536,1024]{1,0:T(8,128)(2,1)S(1)} %copy-done.33), kind=kOutput, calls=%fused_computation.16 | convolution fusion | flops 6444548096 | bytes 13631488 | tf_op jit(solution)/shard_map/dot_general | solution.py:22
  406.6 7.6 %collective-permute-done.60 = bf16[96,2048]{1,0:T(8,128)(2,1)S(1)} collective-permute-done((bf16[96,2048]{1,0:T(8,128)(2,1)S(1)}, bf16[96,2048]{1,0:T(8,128)(2,1)S(1)}, u32[]{:S(2)}, u32[]{:S(2)}) %collective-permute-start.60) | collective-permute-done | bytes 393248 | tf_op jit(solution)/shard_map/ppermute | solution.py:50
  434.4 9.6 %convolution_convert_fusion.7 = bf16[2048,768]{1,0:T(8,128)(2,1)} fusion(bf16[1536,2048]{1,0:T(8,128)(2,1)} %constant_dynamic-update-slice_fusion, bf16[1536,768]{1,0:T(8,128)(2,1)S(1)} %bitcast_dynamic-update-slice_fusion), kind=kOutput, calls=%fused_computation.18 | convolution fusion | flops 4833411072 | bytes 11796480 | tf_op jit(solution)/shard_map/dot_general | solution.py:22
  454.7 12.8 %convolution_convert_fusion.4 = bf16[1024,2048]{1,0:T(8,128)(2,1)} fusion(bf16[1536,2048]{1,0:T(8,128)(2,1)} %copy-done.23, f32[1536,1024]{1,0:T(8,128)} %fusion.75), kind=kOutput, calls=%fused_computation.15 | convolution fusion | flops 6458703872 | bytes 16777216 | tf_op jit(solution)/shard_map/dot_general | solution.py:22
  467.5 7.3 %convolution_convert_fusion = bf16[1536,2048]{1,0:T(8,128)(2,1)S(1)} fusion(bf16[1536,768]{1,0:T(8,128)(2,1)S(1)} %bitcast_dynamic-update-slice_fusion, bf16[2048,768]{1,0:T(8,128)(2,1)} %all-gather.5.cloned.1.call-done), kind=kOutput, calls=%fused_computation.3 | convolution fusion | flops 4834983936 | bytes 11796480 | tf_op jit(solution)/shard_map/dot_general | solution.py:28
  494.1 10.9 %collective-permute-done.69 = bf16[96,2048]{1,0:T(8,128)(2,1)S(1)} collective-permute-done((bf16[96,2048]{1,0:T(8,128)(2,1)S(1)}, bf16[96,2048]{1,0:T(8,128)(2,1)S(1)}, u32[]{:S(2)}, u32[]{:S(2)}) %collective-permute-start.69) | collective-permute-done | bytes 393248 | tf_op jit(solution)/shard_map/ppermute | solution.py:50
  519.8 9.6 %all_to_all.43 = f32[32,1,128]{2,1,0:T(1,128)S(1)} all-to-all(f32[32,1,128]{2,1,0:T(1,128)S(1)} %reshape.387), channel_id=1, replica_groups=mesh['z'=4,'y'=2,'x'=2,'c'=2] {'z','y','x','c'}, dimensions={0} | all-to-all | bytes 32768 | tf_op jit(solution)/shard_map/all_to_all | solution.py:230
  534.3 13.9 %all-to-all-done.7 = bf16[8,64,1024]{2,1,0:T(8,128)(2,1)S(1)} async-done(((bf16[8,64,1024]{2,1,0:T(8,128)(2,1)}), bf16[8,64,1024]{2,1,0:T(8,128)(2,1)S(1)}, u32[]{:S(2)}, u32[]{:S(2)}) %all-to-all-start.7) | async-done | bytes 1048608 | tf_op jit(solution)/shard_map/all_to_all | solution.py:237
  557.7 9.5 %reduce-scatter.7.cloned.1.call-done = bf16[64,2048]{1,0:T(8,128)(2,1)} async-done(((bf16[256,2048]{1,0:T(8,128)(2,1)}), bf16[64,2048]{1,0:T(8,128)(2,1)}) %reduce-scatter.7.cloned.1.call-update) | async-done | bytes 262160 | tf_op jit(solution)/shard_map/reduce_scatter | solution.py:93
  568.9 75.9 %reduce-scatter.11.cloned.1.call-done = bf16[256,2048]{1,0:T(8,128)(2,1)} async-done(((bf16[1024,2048]{1,0:T(8,128)(2,1)}), bf16[256,2048]{1,0:T(8,128)(2,1)}) %reduce-scatter.11.cloned.1.call-update) | async-done | bytes 1048592 | tf_op jit(solution)/shard_map/reduce_scatter | solution.py:93
  (405 shorter events, 298.1 us)
Async XLA Ops:
  7.2 93.0 %all-gather.7.cloned.1.call-start = ((), (), s32[]{:S(2)}) async-start(), calls=%async_computation.13 | async-start | bytes 1310720 | tf_op jit(solution)/shard_map/all_gather | solution.py:89
  7.9 109.7 %all-gather.5.cloned.1.call-start = ((), (), s32[]{:S(2)}) async-start(), calls=%async_computation.12 | async-start | bytes 3932160 | tf_op jit(solution)/shard_map/all_gather | solution.py:89
  36.3 107.8 %collective-permute-start.39 = (bf16[192,2048]{1,0:T(8,128)(2,1)}, bf16[192,2048]{1,0:T(8,128)(2,1)}, u32[]{:S(2)}, u32[]{:S(2)}) collective-permute-start(bf16[192,2048]{1,0:T(8,128)(2,1)} %get-tuple-element.24), channel_id=1, source_target_pairs={{0,4},{4,0},{1,5},{5,1},{2,6},{6,2},{3,7},{7,3},{8,12},{12,8},{9,1... | collective-permute-start | bytes 2359304 | tf_op jit(solution)/shard_map/ppermute | solution.py:50
  42.5 48.5 %all-to-all-start.3 = ((bf16[8,64,1024]{2,1,0:T(8,128)(2,1)}), bf16[8,64,1024]{2,1,0:T(8,128)(2,1)S(1)}, u32[]{:S(2)}, u32[]{:S(2)}) async-start(bf16[8,64,1024]{2,1,0:T(8,128)(2,1)} %reshape.350), calls=%async_computation.3 | async-start | bytes 2097152 | tf_op jit(solution)/shard_map/all_to_all | solution.py:148
  46.1 188.5 %all-gather.9.cloned.1.call-start = ((), (), s32[]{:S(2)}) async-start(), calls=%async_computation.14 | async-start | bytes 5242880 | tf_op jit(solution)/shard_map/all_gather | solution.py:89
  47.6 29.8 %collective-permute-start.1 = (bf16[192,2048]{1,0:T(8,128)(2,1)S(1)}, bf16[192,2048]{1,0:T(8,128)(2,1)S(1)}, u32[]{:S(2)}, u32[]{:S(2)}) collective-permute-start(bf16[192,2048]{1,0:T(8,128)(2,1)S(1)} %get-tuple-element.30), channel_id=1, source_target_pairs={{0,2},{2,0},{1,3},{3,1},{4,6},{6,4},{5,7},{7,5},{8,10},{10,8},{9,1... | collective-permute-start | bytes 2359304 | tf_op jit(solution)/shard_map/ppermute | solution.py:50
  49.4 35.1 %collective-permute-start.3 = (bf16[192,2048]{1,0:T(8,128)(2,1)S(1)}, bf16[192,2048]{1,0:T(8,128)(2,1)S(1)}, u32[]{:S(2)}, u32[]{:S(2)}) collective-permute-start(bf16[192,2048]{1,0:T(8,128)(2,1)S(1)} %get-tuple-element.30), channel_id=1, source_target_pairs={{0,4},{4,0},{1,5},{5,1},{2,6},{6,2},{3,7},{7,3},{8,12},{12,8},{9,1... | collective-permute-start | bytes 2359304 | tf_op jit(solution)/shard_map/ppermute | solution.py:50
  50.9 38.1 %collective-permute-start = (bf16[192,2048]{1,0:T(8,128)(2,1)S(1)}, bf16[192,2048]{1,0:T(8,128)(2,1)S(1)}, u32[]{:S(2)}, u32[]{:S(2)}) collective-permute-start(bf16[192,2048]{1,0:T(8,128)(2,1)S(1)} %get-tuple-element.30), channel_id=1, source_target_pairs={{0,1},{1,0},{2,3},{3,2},{4,5},{5,4},{6,7},{7,6},{8,9},{9,8},{10,11... | collective-permute-start | bytes 2359304 | tf_op jit(solution)/shard_map/ppermute | solution.py:50
  77.4 28.8 %collective-permute-start.2 = (bf16[192,2048]{1,0:T(8,128)(2,1)S(1)}, bf16[192,2048]{1,0:T(8,128)(2,1)}, u32[]{:S(2)}, u32[]{:S(2)}) collective-permute-start(bf16[192,2048]{1,0:T(8,128)(2,1)S(1)} %collective-permute-done.1), channel_id=1, source_target_pairs={{0,1},{1,0},{2,3},{3,2},{4,5},{5,4},{6,7},{7,6},{8,9},{9,8},{10,11... | collective-permute-start | bytes 2359304 | tf_op jit(solution)/shard_map/ppermute | solution.py:50
  92.0 175.6 %all-gather.11.cloned.1.call-start = ((), (), s32[]{:S(2)}) async-start(), calls=%async_computation.15 | async-start | bytes 5242880 | tf_op jit(solution)/shard_map/all_gather | solution.py:89
  96.2 49.5 %collective-permute-start.37 = (bf16[192,2048]{1,0:T(8,128)(2,1)}, bf16[192,2048]{1,0:T(8,128)(2,1)}, u32[]{:S(2)}, u32[]{:S(2)}) collective-permute-start(bf16[192,2048]{1,0:T(8,128)(2,1)} %get-tuple-element.24), channel_id=1, source_target_pairs={{0,2},{2,0},{1,3},{3,1},{4,6},{6,4},{5,7},{7,5},{8,10},{10,8},{9,1... | collective-permute-start | bytes 2359304 | tf_op jit(solution)/shard_map/ppermute | solution.py:50
  143.6 385.8 %reduce-scatter.9.cloned.1.call-start = ((), (), s32[]{:S(2)}) async-start(), calls=%async_computation.18 | async-start | bytes 5242880 | tf_op jit(solution)/shard_map/reduce_scatter | solution.py:93
  145.7 32.7 %collective-permute-start.42 = (bf16[96,2048]{1,0:T(8,128)(2,1)S(1)}, bf16[96,2048]{1,0:T(8,128)(2,1)S(1)}, u32[]{:S(2)}, u32[]{:S(2)}) collective-permute-start(bf16[96,2048]{1,0:T(8,128)(2,1)S(1)} %slice.379), channel_id=1, source_target_pairs={{0,2},{2,0},{1,3},{3,1},{4,6},{6,4},{5,7},{7,5},{8,10},{10,8},{9,1... | collective-permute-start | bytes 1179656 | tf_op jit(solution)/shard_map/ppermute | solution.py:50
  147.3 32.6 %collective-permute-start.41 = (bf16[96,2048]{1,0:T(8,128)(2,1)S(1)}, bf16[96,2048]{1,0:T(8,128)(2,1)S(1)}, u32[]{:S(2)}, u32[]{:S(2)}) collective-permute-start(bf16[96,2048]{1,0:T(8,128)(2,1)S(1)} %slice.378), channel_id=1, source_target_pairs={{0,4},{4,0},{1,5},{5,1},{2,6},{6,2},{3,7},{7,3},{8,12},{12,8},{9,1... | collective-permute-start | bytes 1179656 | tf_op jit(solution)/shard_map/ppermute | solution.py:50
  148.9 31.6 %collective-permute-start.38 = (bf16[192,2048]{1,0:T(8,128)(2,1)}, bf16[192,2048]{1,0:T(8,128)(2,1)S(1)}, u32[]{:S(2)}, u32[]{:S(2)}) collective-permute-start(bf16[192,2048]{1,0:T(8,128)(2,1)} %collective-permute-done.37), channel_id=1, source_target_pairs={{0,1},{1,0},{2,3},{3,2},{4,5},{5,4},{6,7},{7,6},{8,9},{9,8},{10,11... | collective-permute-start | bytes 2359304 | tf_op jit(solution)/shard_map/ppermute | solution.py:50
  153.8 27.4 %collective-permute-start.8 = (bf16[192,2048]{1,0:T(8,128)(2,1)S(1)}, bf16[192,2048]{1,0:T(8,128)(2,1)S(1)}, u32[]{:S(2)}, u32[]{:S(2)}) collective-permute-start(bf16[192,2048]{1,0:T(8,128)(2,1)S(1)} %get-tuple-element.52), channel_id=1, source_target_pairs={{0,1},{1,0},{2,3},{3,2},{4,5},{5,4},{6,7},{7,6},{8,9},{9,8},{10,11... | collective-permute-start | bytes 2359304 | tf_op jit(solution)/shard_map/ppermute | solution.py:50
  291.1 65.5 %collective-permute-start.44 = (bf16[192,2048]{1,0:T(8,128)(2,1)S(1)}, bf16[192,2048]{1,0:T(8,128)(2,1)S(1)}, u32[]{:S(2)}, u32[]{:S(2)}) collective-permute-start(bf16[192,2048]{1,0:T(8,128)(2,1)S(1)} %get-tuple-element.38), channel_id=1, source_target_pairs={{0,1},{1,0},{2,3},{3,2},{4,5},{5,4},{6,7},{7,6},{8,9},{9,8},{10,11... | collective-permute-start | bytes 2359304 | tf_op jit(solution)/shard_map/ppermute | solution.py:50
  305.1 53.0 %collective-permute-start.26 = (bf16[192,2048]{1,0:T(8,128)(2,1)S(1)}, bf16[192,2048]{1,0:T(8,128)(2,1)S(1)}, u32[]{:S(2)}, u32[]{:S(2)}) collective-permute-start(bf16[192,2048]{1,0:T(8,128)(2,1)S(1)} %get-tuple-element.51), channel_id=1, source_target_pairs={{0,1},{1,0},{2,3},{3,2},{4,5},{5,4},{6,7},{7,6},{8,9},{9,8},{10,11... | collective-permute-start | bytes 2359304 | tf_op jit(solution)/shard_map/ppermute | solution.py:50
  306.8 51.6 %collective-permute-start.53 = (bf16[96,2048]{1,0:T(8,128)(2,1)S(1)}, bf16[96,2048]{1,0:T(8,128)(2,1)S(1)}, u32[]{:S(2)}, u32[]{:S(2)}) collective-permute-start(bf16[96,2048]{1,0:T(8,128)(2,1)S(1)} %slice.477), channel_id=1, source_target_pairs={{0,4},{4,0},{1,5},{5,1},{2,6},{6,2},{3,7},{7,3},{8,12},{12,8},{9,1... | collective-permute-start | bytes 1179656 | tf_op jit(solution)/shard_map/ppermute | solution.py:50
  308.3 50.7 %collective-permute-start.46 = (bf16[96,2048]{1,0:T(8,128)(2,1)S(1)}, bf16[96,2048]{1,0:T(8,128)(2,1)S(1)}, u32[]{:S(2)}, u32[]{:S(2)}) collective-permute-start(bf16[96,2048]{1,0:T(8,128)(2,1)S(1)} %slice.478), channel_id=1, source_target_pairs={{0,2},{2,0},{1,3},{3,1},{4,6},{6,4},{5,7},{7,5},{8,10},{10,8},{9,1... | collective-permute-start | bytes 1179656 | tf_op jit(solution)/shard_map/ppermute | solution.py:50
  399.8 148.4 %reduce-scatter.5.cloned.1.call-start = ((), (), s32[]{:S(2)}) async-start(), calls=%async_computation.16 | async-start | bytes 3932160 | tf_op jit(solution)/shard_map/reduce_scatter | solution.py:93
  444.0 123.1 %reduce-scatter.7.cloned.1.call-start = ((), (), s32[]{:S(2)}) async-start(), calls=%async_computation.17 | async-start | bytes 1310720 | tf_op jit(solution)/shard_map/reduce_scatter | solution.py:93
  454.6 190.2 %reduce-scatter.11.cloned.1.call-start = ((), (), s32[]{:S(2)}) async-start(), calls=%async_computation.19 | async-start | bytes 5242880 | tf_op jit(solution)/shard_map/reduce_scatter | solution.py:93
  548.3 104.0 %all-to-all-start.5 = ((bf16[8,64,768]{2,1,0:T(8,128)(2,1)}), bf16[8,64,768]{2,1,0:T(8,128)(2,1)}, u32[]{:S(2)}, u32[]{:S(2)}) async-start(bf16[8,64,768]{2,1,0:T(8,128)(2,1)} %bitcast.168), calls=%async_computation.6 | async-start | bytes 1572864 | tf_op jit(solution)/shard_map/all_to_all | solution.py:240
  (96 other events, 1177.6 us)
Sparse Core Ops, SparseCore 0:
  9.6 31.5 all-gather.6
  42.8 62.5 all-gather.4
  107.5 79.3 all-gather.8
  188.3 79.2 all-gather.10
  400.0 74.2 reduce-scatter.8
  476.4 61.1 reduce-scatter.4
  539.9 27.1 reduce-scatter.6
  569.4 75.3 reduce-scatter.10

commit v2 on v1

v2 whole, which is shorter than its diff:
```python
import jax
import jax.numpy as jnp
from jax import lax
from jax.experimental import pallas as pl
from jax.experimental.pallas import tpu as pltpu
from jax.sharding import Mesh, PartitionSpec as P

H = 16
HD = 128
IMAGE = 144
EPSILON = 1e-05
NEG_LARGE = -1e30

ALL = ("z", "y", "x", "c")
TEAM = ("y", "x", "c")
SWAP = [(0, 1), (1, 0)]


def matmul(left_side, right_side):
    return jnp.dot(left_side, right_side, preferred_element_type=jnp.float32)


def gram_rows(left_side, right_side):
    return lax.dot_general(
        left_side, right_side, (((0,), (0,)), ((), ())), preferred_element_type=jnp.float32
    )


def times_transposed(left_side, right_side):
    return lax.dot_general(
        left_side, right_side, (((1,), (1,)), ((), ())), preferred_element_type=jnp.float32
    )


def gelu_tanh(values):
    return jax.nn.gelu(values, approximate=True)


def norm_stats(values):
    center = values - jnp.mean(values, axis=-1, keepdims=True)
    inverse = lax.rsqrt(jnp.mean(center * center, axis=-1, keepdims=True) + EPSILON)
    return (center * inverse, inverse)


def norm_backward(grad_scaled, scaled, inverse):
    first_mean = jnp.mean(grad_scaled, axis=-1, keepdims=True)
    second_mean = jnp.mean(grad_scaled * scaled, axis=-1, keepdims=True)
    return inverse * (grad_scaled - first_mean - scaled * second_mean)


FIRST = (2, 4)
SECOND = (4, 2)
ORDER = ((0, 2, 4, 6, 1, 5, 3, 7), (0, 4, 2, 6, 1, 3, 5, 7))


def first_hop(block):
    return lax.ppermute(block, TEAM, [(t, t ^ FIRST[t & 1]) for t in range(8)])


def second_hop(block):
    return lax.ppermute(block, TEAM, [(t, t ^ SECOND[t & 1]) for t in range(8)])


def core_hop(block):
    return lax.ppermute(block, TEAM, [(t, t ^ 1) for t in range(8)])


def after(value, *others):
    return lax.optimization_barrier((value, *others))[0]


def team_gather(block, *others):
    near = first_hop(block)
    if others:
        near = after(near, *others)
    pair = jnp.concatenate([block, near], axis=0)
    other = second_hop(pair)
    return jnp.concatenate([pair, other, core_hop(pair), core_hop(other)], axis=0)


def team_sum(terms_of, rows, held=None, beside=None):
    low = jnp.bfloat16
    half = rows.shape[0] // 2
    quarter = half // 2
    arrived = core_hop(terms_of(rows[half:]).astype(low))
    near = terms_of(rows[:half]) + arrived.astype(jnp.float32)
    if beside is not None:
        held = after(held, arrived)
    far = second_hop(near[quarter:].astype(low))
    near = near[:quarter] + far.astype(jnp.float32)
    last = first_hop(near[quarter // 2 :].astype(low))
    if beside is None:
        return near[: quarter // 2] + last.astype(jnp.float32)
    result = beside(held)
    last, result = lax.optimization_barrier((last, result))
    return near[: quarter // 2] + last.astype(jnp.float32), result


def meet(kept, sent):
    arrived = core_hop(sent)
    core = lax.axis_index("c")
    return jnp.stack([jnp.where(core == 0, kept, arrived), jnp.where(core == 0, arrived, kept)], axis=1)


def own_part(parts):
    core = lax.axis_index("c")
    return jnp.where(core == 0, parts[0], parts[1]), jnp.where(core == 0, parts[1], parts[0])


def weight_gather(block):
    return lax.all_gather(block, "z", axis=0, tiled=True)


def weight_scatter(terms):
    return lax.psum_scatter(terms.astype(jnp.bfloat16), "z", scatter_dimension=0, tiled=True)


def probs_of(item_lengths, qkv, head, width):
    slots = qkv.shape[0]
    queries = qkv[:, head * HD : (head + 1) * HD]
    key_rows = qkv[:, width + head * HD : width + (head + 1) * HD]
    value_rows = qkv[:, 2 * width + head * HD : 2 * width + (head + 1) * HD]
    row = lax.broadcasted_iota(jnp.int32, (slots, slots), 0)
    col = lax.broadcasted_iota(jnp.int32, (slots, slots), 1)
    allowed = (col <= row) & (col < item_lengths[pl.program_id(0)])
    masked = jnp.where(allowed, times_transposed(queries, key_rows) * HD ** (-0.5), NEG_LARGE)
    shifted = jnp.exp(masked - jnp.max(masked, axis=-1, keepdims=True))
    return queries, key_rows, value_rows, shifted / jnp.sum(shifted, axis=-1, keepdims=True)


def attend_kernel(item_lengths, qkv, mixed):
    width = mixed.shape[1]
    for head in range(width // HD):
        _, _, value_rows, probs = probs_of(item_lengths, qkv, head, width)
        own = matmul(probs.astype(mixed.dtype), value_rows)
        mixed[:, head * HD : (head + 1) * HD] = own.astype(mixed.dtype)


def attend_back_kernel(item_lengths, qkv, grad_mixed, grad_qkv):
    width = grad_mixed.shape[1]
    low = grad_qkv.dtype
    score_scale = HD ** (-0.5)
    for head in range(width // HD):
        queries, key_rows, value_rows, probs = probs_of(item_lengths, qkv, head, width)
        grad_own = grad_mixed[:, head * HD : (head + 1) * HD]
        grad_probs = times_transposed(grad_own, value_rows)
        row_delta = jnp.sum(probs * grad_probs, axis=-1, keepdims=True)
        grad_scores = (probs * (grad_probs - row_delta)).astype(low)
        at = head * HD
        grad_qkv[:, at : at + HD] = (matmul(grad_scores, key_rows) * score_scale).astype(low)
        at += width
        grad_qkv[:, at : at + HD] = (gram_rows(grad_scores, queries) * score_scale).astype(low)
        at += width
        grad_qkv[:, at : at + HD] = gram_rows(probs.astype(low), grad_own).astype(low)


def attend_call(kernel, name, slots, lengths, operands, width, products):
    rows = operands[0].shape[0]
    own = operands[-1].shape[1] if products > 2 else width
    size = 2 * rows * slots * HD * products * (own // HD)

    def spec(columns):
        return pl.BlockSpec((slots, columns), lambda item, _: (item, 0))

    return pl.pallas_call(
        kernel,
        out_shape=jax.ShapeDtypeStruct((rows, width), operands[0].dtype),
        grid_spec=pltpu.PrefetchScalarGridSpec(
            num_scalar_prefetch=1,
            grid=(rows // slots,),
            in_specs=[spec(operand.shape[1]) for operand in operands],
            out_specs=spec(width),
        ),
        cost_estimate=pl.CostEstimate(
            flops=size,
            bytes_accessed=2 * rows * (width + sum(operand.shape[1] for operand in operands)),
            transcendentals=rows * slots * (own // HD),
        ),
        name=name,
    )(lengths, *operands)


def per_device(
    inputs, counts, gain_attn, w_query, w_key, w_value, w_out, gain_mlp, w_up, w_down, cotangent
):
    low = jnp.bfloat16
    layers = lax.axis_size("z")
    team = lax.axis_size(TEAM)
    devices = layers * team
    item_count, slot_count, features = inputs.shape
    assert item_count == 1
    row_count = item_count * slot_count
    wide_rows = row_count * team
    depth = w_query.shape[0]
    head_parts = HD // depth
    head_axes = TEAM[len(TEAM) - (head_parts.bit_length() - 1) :]
    head_groups = team // head_parts
    own_heads = layers // head_parts
    own_width = own_heads * HD
    units = w_down.shape[0]
    own_units = layers * units

    def own_columns(weight):
        cut = weight.reshape(depth, head_parts, own_heads, head_groups, HD)
        return cut.transpose(3, 1, 0, 2, 4).reshape(team, depth, own_width)

    qkv_cut = jnp.concatenate([own_columns(w_query), own_columns(w_key), own_columns(w_value)], axis=2)
    qkv_cut = lax.all_to_all(qkv_cut, TEAM, 0, 0, tiled=True).reshape(team * depth, 3 * own_width)
    strip = features // team
    out_cut = w_out.reshape(depth, team, strip).transpose(1, 0, 2).reshape(team * depth, strip)
    w_attn = weight_gather(jnp.concatenate([qkv_cut, out_cut], axis=1))
    up_cut = w_up.reshape(depth, layers, team, units).transpose(2, 0, 1, 3)
    up_cut = lax.all_to_all(up_cut.reshape(team, depth, own_units), TEAM, 0, 0, tiled=True)
    up_cut = up_cut.reshape(team * depth, own_units)
    strips = features // own_units
    down_cut = w_down.reshape(units, strips, own_units).transpose(1, 0, 2)
    down_cut = down_cut.reshape(team * depth, own_units)
    w_mlp = weight_gather(jnp.concatenate([up_cut, down_cut], axis=1))

    small = jnp.stack(
        [gain_attn, gain_mlp, jnp.broadcast_to(counts.astype(low)[:1], gain_attn.shape)], axis=0
    )
    small = lax.all_to_all(
        jnp.broadcast_to(small[None], (devices,) + small.shape), ALL, 0, 0, tiled=True
    )
    full_gain_a = small[:, 0].reshape(1, features).astype(jnp.float32)
    full_gain_m = small[:, 1].reshape(1, features).astype(jnp.float32)
    member = lax.axis_index("z") * team + (lax.axis_index(TEAM) ^ jnp.array(ORDER)[lax.axis_index("c")])
    picked = member[:, None] == jnp.arange(devices)[None, :]
    team_counts = jnp.sum(jnp.where(picked, small[:, 2, 0].astype(jnp.float32)[None, :], 0.0), axis=1)
    team_lengths = team_counts.astype(jnp.int32) + IMAGE

    stream = inputs.reshape(row_count, features).astype(jnp.float32)
    scaled_a, inverse_a = norm_stats(stream)
    normed_a = team_gather((scaled_a * full_gain_a).astype(low))

    position = jnp.arange(slot_count)
    lengths = counts + IMAGE
    live = (position[None, :] < lengths[:, None]).reshape(row_count, 1)
    cotangent_low = jnp.where(live, cotangent.reshape(row_count, features), jnp.zeros((), low))
    grad_stream = cotangent_low.astype(jnp.float32)
    grad_low = team_gather(cotangent_low)
    normed_a = after(normed_a, up_cut, grad_low)

    w_qkv = w_attn[:, : 3 * own_width]
    qkv = matmul(normed_a, w_qkv).astype(low)
    out_rows = w_attn[:, 3 * own_width :].reshape(layers, team, depth, strip)
    out_rows = out_rows.transpose(0, 2, 1, 3).reshape(layers, depth, features)
    if head_parts == 2:
        w_out_own = meet(*own_part(out_rows.reshape(2, own_heads, depth, features)))
    else:
        out_rows = out_rows.reshape(head_parts, own_heads, depth, features)
        w_out_own = lax.all_to_all(out_rows, head_axes, 0, 0, tiled=True).transpose(1, 0, 2, 3)
    w_out_own = w_out_own.reshape(own_width, features)
    mixed = attend_call(attend_kernel, "attend", slot_count, team_lengths, (qkv,), own_width, 2)
    residual = stream + team_sum(lambda rows: matmul(rows, w_out_own), mixed)

    scaled_m, inverse_m = norm_stats(residual)
    normed_m = team_gather((scaled_m * full_gain_m).astype(low))
    w_up_own = w_mlp[:, :own_units]
    w_down_own = w_mlp[:, own_units:].reshape(layers, strips, units, own_units)
    w_down_own = w_down_own.transpose(0, 2, 1, 3).reshape(own_units, features)
    hidden = matmul(normed_m, w_up_own)
    gelu_value, gelu_back = jax.vjp(gelu_tanh, hidden)
    active = gelu_value.astype(low)

    grad_down = gram_rows(active, grad_low).astype(low)
    grad_down, grad_low = lax.optimization_barrier((grad_down, grad_low))
    grad_down = weight_scatter(grad_down)
    grad_active = times_transposed(grad_low, w_down_own)
    grad_hidden = gelu_back(grad_active)[0].astype(low)
    grad_normed_m, grad_up = team_sum(
        lambda rows: times_transposed(rows, w_up_own),
        grad_hidden,
        grad_hidden,
        lambda held: gram_rows(normed_m, held).astype(low),
    )
    grad_up = weight_scatter(grad_up)
    gain_m_terms = jnp.sum(grad_normed_m * scaled_m, axis=0)
    grad_residual = norm_backward(grad_normed_m * full_gain_m, scaled_m, inverse_m) + grad_stream

    grad_residual_low = team_gather(grad_residual.astype(low))
    grad_mixed = times_transposed(grad_residual_low, w_out_own).astype(low)
    grad_qkv = attend_call(
        attend_back_kernel, "attend_back", slot_count, team_lengths, (qkv, grad_mixed), 3 * own_width, 6
    )
    grad_out = gram_rows(mixed, grad_residual_low).astype(low)
    grad_out = grad_out.reshape(own_heads, head_parts, depth, features).transpose(1, 0, 2, 3)
    if head_parts == 2:
        kept, sent = own_part(grad_out)
        arrived = core_hop(sent)
        core = lax.axis_index("c")
        grad_out = jnp.concatenate(
            [jnp.where(core == 0, kept, arrived), jnp.where(core == 0, arrived, kept)], axis=0
        )
    else:
        grad_out = lax.all_to_all(grad_out, head_axes, 0, 0, tiled=True)
    grad_out = grad_out.reshape(layers, depth, team, strip).transpose(0, 2, 1, 3)
    grad_out = grad_out.reshape(features, strip)
    grad_qkv_w = gram_rows(normed_a, grad_qkv).astype(low)
    grad_attn = weight_scatter(jnp.concatenate([grad_qkv_w, grad_out], axis=1))
    grad_qkv_w = grad_attn[:, : 3 * own_width]
    grad_out = grad_attn[:, 3 * own_width :].reshape(team, depth, strip)
    grad_out = grad_out.transpose(1, 0, 2).reshape(depth, features)
    grad_normed_a = team_sum(lambda rows: times_transposed(rows, w_qkv), grad_qkv)
    active = after(active, grad_qkv)
    output = residual + team_sum(lambda rows: matmul(rows, w_down_own), active)
    gain_a_terms = jnp.sum(grad_normed_a * scaled_a, axis=0)
    grad_input = norm_backward(grad_normed_a * full_gain_a, scaled_a, inverse_a) + grad_residual

    gain_terms = jnp.stack([gain_a_terms, gain_m_terms], axis=0).reshape(2, devices, depth)
    gain_terms = lax.all_to_all(gain_terms.transpose(1, 0, 2), ALL, 0, 0, tiled=True)
    gain_grads = jnp.sum(gain_terms, axis=0)

    def all_columns(cut):
        cut = cut.reshape(head_groups, head_parts, depth, own_heads, HD)
        return cut.transpose(2, 1, 3, 0, 4).reshape(depth, features).astype(jnp.float32)

    grad_up = lax.all_to_all(grad_up.reshape(team, depth, own_units), TEAM, 0, 0, tiled=True)
    grad_up = grad_up.reshape(team, depth, layers, units).transpose(1, 2, 0, 3)
    grad_up = grad_up.reshape(depth, layers * team * units).astype(jnp.float32)
    back = lax.all_to_all(grad_qkv_w.reshape(team, depth, 3 * own_width), TEAM, 0, 0, tiled=True)

    return (
        output.reshape(item_count, slot_count, features).astype(low),
        grad_input.reshape(item_count, slot_count, features),
        gain_grads[0],
        all_columns(back[:, :, :own_width]),
        all_columns(back[:, :, own_width : 2 * own_width]),
        all_columns(back[:, :, 2 * own_width :]),
        grad_out.astype(jnp.float32),
        gain_grads[1],
        grad_up,
        grad_down.astype(jnp.float32),
    )


def solution(mesh):
    wide, narrow = mesh.shape["wide"], mesh.shape["narrow"]
    steps = Mesh(mesh.devices.reshape(wide // 2, 2, narrow // 2, 2), ALL)
    rows, items = P(ALL, None), P(ALL, None, None)
    return jax.shard_map(
        per_device,
        mesh=steps,
        in_specs=(items, P(ALL), P(ALL), rows, rows, rows, rows, P(ALL), rows, rows, items),
        out_specs=(items, items, P(ALL), rows, rows, rows, rows, P(ALL), rows, rows),
        check_vma=False,
    )
```

time: 672 us -> 654 us (0.973)
  blocking collectives: 38.6 us -> 0 us
  local copies, waits for them, and re-layouts: 75.7 us -> 107 us
  Pallas kernels: 0 us -> 22.3 us
  starting transfers between devices: 67.8 us -> 49.5 us
  waiting for transfers between devices: 315 us -> 298 us
    all_to_all x4 -> x0, blocking collectives: 38.6 us -> none  [the longest x1 17.8 us: per_device(): qkv_cut = lax.all_to_all(qkv_cut, TEAM, 0, 0, tiled=True)]
    ppermute x72 -> x30, waiting for transfers between devices: 192 us -> 163 us  [the longest x8 102 us: second_hop(): return lax.ppermute(block, TEAM, [(t, t ^ SECOND[t & 1]) for t in range(8)])]
    ppermute x72 -> x30, starting transfers between devices: 51 us -> 24.6 us  [the longest x8 11 us: second_hop(): return lax.ppermute(block, TEAM, [(t, t ^ SECOND[t & 1]) for t in range(8)])]
    pallas_call x0 -> x2, Pallas kernels: none -> 22.3 us  [attend_call(): pl.pallas_call(kernel, out_shape=jax.ShapeDtypeStruct((rows, width), oper...]
    unnamed x106 -> x112, local copies, waits for them, and re-layouts: 37.2 us -> 52.4 us
    all_to_all x1, waiting for transfers between devices: 13.9 us -> 0.01 us  [per_device(): lax.all_to_all(grad_up.reshape(team, depth, own_units), TEAM, 0, 0, tiled...]
    all_gather x4 -> x2, waiting for transfers between devices: 21.2 us -> 34.2 us  [weight_gather(): return lax.all_gather(block, 'z', axis=0, tiled=True)]
    reduce_scatter x4 -> x3, waiting for transfers between devices: 85.3 us -> 72.4 us  [weight_scatter(): lax.psum_scatter(terms.astype(jnp.bfloat16), 'z', scatter_dimension=0, ti...]
  transfers between devices with their start and end apart: 84 -> 41, of which waited for: 38 -> 21; matrix products, arithmetic and copies ran while one was open for 28% -> 28% of each run, Pallas kernels for 0% -> 3%
where the time goes in v2:
time: 654 us; the launch traced here: 645 us
  waiting for transfers between devices  298 us (46%)
  local copies, waits for them, and re-layouts  107 us (16%)
  matrix products  104 us (16%)
  starting transfers between devices  49.5 us (8%)
  other arithmetic  47.6 us (7%)
  Pallas kernels  22.3 us (3%)
  between operations  15.8 us (2%)
    ppermute x8, waiting for transfers between devices, second_hop(): return lax.ppermute(block, TEAM, [(t, t ^ SECOND[t & 1]) for t in range(8)])  102 us
    reduce_scatter x3, waiting for transfers between devices, weight_scatter(): lax.psum_scatter(terms.astype(jnp.bfloat16), 'z', scatter_dimension=0, ti...  72.4 us
    unnamed x112, local copies, waits for them, and re-layouts  52.4 us
    ppermute x8, waiting for transfers between devices, first_hop(): return lax.ppermute(block, TEAM, [(t, t ^ FIRST[t & 1]) for t in range(8)])  49.7 us
    dot_general x6, matrix products, times_transposed(): lax.dot_general(left_side, right_side, (((1,), (1,)), ((), ())), preferre...  40.1 us
    all_gather x2, waiting for transfers between devices, weight_gather(): return lax.all_gather(block, 'z', axis=0, tiled=True)  34.2 us
    dot_general x6, matrix products, matmul(): return jnp.dot(left_side, right_side, preferred_element_type=jnp.float32)  32.7 us
    dot_general x4, matrix products, gram_rows(): lax.dot_general(left_side, right_side, (((0,), (0,)), ((), ())), preferre...  31.6 us
  transfers between devices with their start and end apart: 41, of which 21 were waited for; matrix products, arithmetic and copies ran while one was open for 28% of the time, Pallas kernels for 3%

profile of v2, /device:TPU:0, one launch (start us, length us, event | category | flops | bytes accessed | tf_op | source)
XLA Modules:
  0.0 645.0 jit_solution(13562938358753244518)
XLA Ops:
  17.3 12.4 %all-to-all-done.2 = bf16[8,64,768]{2,1,0:T(8,128)(2,1)S(1)} async-done(((bf16[8,64,768]{2,1,0:T(8,128)(2,1)}), bf16[8,64,768]{2,1,0:T(8,128)(2,1)S(1)}, u32[]{:S(2)}, u32[]{:S(2)}) %all-to-all-start.2) | async-done | bytes 786464 | tf_op jit(solution)/shard_map/all_to_all | solution.py:208
  52.6 10.0 %collective-permute-done = bf16[192,2048]{1,0:T(8,128)(2,1)S(1)} collective-permute-done((bf16[192,2048]{1,0:T(8,128)(2,1)S(1)}, bf16[192,2048]{1,0:T(8,128)(2,1)S(1)}, u32[]{:S(2)}, u32[]{:S(2)}) %collective-permute-start) | collective-permute-done | bytes 786464 | tf_op jit(solution)/shard_map/ppermute | solution.py:57
  81.1 15.7 %collective-permute-done.1 = bf16[384,2048]{1,0:T(8,128)(2,1)} collective-permute-done((bf16[384,2048]{1,0:T(8,128)(2,1)}, bf16[384,2048]{1,0:T(8,128)(2,1)}, u32[]{:S(2)}, u32[]{:S(2)}) %collective-permute-start.1) | collective-permute-done | bytes 1572896 | tf_op jit(solution)/shard_map/ppermute | solution.py:61
  97.5 6.6 %all-to-all-done.1 = bf16[8,64,1024]{2,1,0:T(8,128)(2,1)S(1)} async-done(((bf16[8,64,1024]{2,1,0:T(8,128)(2,1)}), bf16[8,64,1024]{2,1,0:T(8,128)(2,1)S(1)}, u32[]{:S(2)}, u32[]{:S(2)}) %all-to-all-start.1) | async-done | bytes 1048608 | tf_op jit(solution)/shard_map/all_to_all | solution.py:213
  125.5 9.2 %convolution_convert_fusion.6.qkv = bf16[1536,768]{1,0:T(8,128)(2,1)} fusion(bf16[1536,2048]{1,0:T(8,128)(2,1)} %constant_dynamic-update-slice_fusion, bf16[2048,1024]{1,0:T(8,128)(2,1)S(1)} %copy-done.24), kind=kOutput, calls=%fused_computation.21 | convolution fusion | flops 4833017856 | bytes 11796480 | tf_op jit(solution)/shard_map/dot_general | solution.py:20
  134.7 9.7 %attend.1 = bf16[1536,256]{1,0:T(8,128)(2,1)} custom-call(s32[8]{0:T(128)} %convert_add_fusion.5.item_lengths, bf16[1536,768]{1,0:T(8,128)(2,1)} %convolution_convert_fusion.6.qkv), custom_call_target="tpu_custom_call" | custom-call | flops 301989888 | bytes 3145728 | tf_op jit(solution)/shard_map/attend/pallas_call | solution.py:165
  155.2 19.9 %collective-permute-done.10 = bf16[384,2048]{1,0:T(8,128)(2,1)S(1)} collective-permute-done((bf16[384,2048]{1,0:T(8,128)(2,1)S(1)}, bf16[384,2048]{1,0:T(8,128)(2,1)S(1)}, u32[]{:S(2)}, u32[]{:S(2)}) %collective-permute-start.10) | collective-permute-done | bytes 1572896 | tf_op jit(solution)/shard_map/ppermute | solution.py:61
  178.4 11.3 %collective-permute-done.11 = bf16[192,2048]{1,0:T(8,128)(2,1)} collective-permute-done((bf16[192,2048]{1,0:T(8,128)(2,1)S(1)}, bf16[192,2048]{1,0:T(8,128)(2,1)}, u32[]{:S(2)}, u32[]{:S(2)}) %collective-permute-start.11) | collective-permute-done | bytes 786464 | tf_op jit(solution)/shard_map/ppermute | solution.py:57
  193.9 11.3 %collective-permute-done.12 = bf16[192,2048]{1,0:T(8,128)(2,1)S(1)} collective-permute-done((bf16[192,2048]{1,0:T(8,128)(2,1)S(1)}, bf16[192,2048]{1,0:T(8,128)(2,1)S(1)}, u32[]{:S(2)}, u32[]{:S(2)}) %collective-permute-start.12) | collective-permute-done | bytes 786464 | tf_op jit(solution)/shard_map/ppermute | solution.py:57
  207.0 20.2 %collective-permute-done.13 = bf16[384,2048]{1,0:T(8,128)(2,1)} collective-permute-done((bf16[384,2048]{1,0:T(8,128)(2,1)}, bf16[384,2048]{1,0:T(8,128)(2,1)}, u32[]{:S(2)}, u32[]{:S(2)}) %collective-permute-start.13) | collective-permute-done | bytes 1572896 | tf_op jit(solution)/shard_map/ppermute | solution.py:61
  227.2 34.2 %all-gather.5.cloned.1.call-done = bf16[2048,2048]{1,0:T(8,128)(2,1)} async-done(((bf16[512,2048]{1,0:T(8,128)(2,1)}), bf16[2048,2048]{1,0:T(8,128)(2,1)}) %all-gather.5.cloned.1.call-update) | async-done | bytes 8388624 | tf_op jit(solution)/shard_map/all_gather | solution.py:111
  266.1 8.5 %copy.98 = bf16[4,2,256,1024]{3,1,2,0:T(2,128)(2,1)} copy(bf16[4,2,256,1024]{3,2,1,0:T(8,128)(2,1)} %bitcast.151) | data formatting | bytes 8388608 | tf_op jit(solution)/shard_map/reshape | solution.py:261
  290.3 11.8 %multiply_convert_fusion = (bf16[1536,1024]{1,0:T(8,128)(2,1)S(1)}, f32[1536,1024]{1,0:T(8,128)}) fusion(bf16[1536,2048]{1,0:T(8,128)(2,1)} %constant_dynamic-update-slice_fusion.10, bf16[2048,2048]{1,0:T(8,128)(2,1)S(1)} %bitcast.174), kind=kOutput, calls=%fused_computation.12 | convolution fusion | flops 6456606720 | bytes 19922944 | tf_op jit(solution)/shard_map/dot_general | solution.py:20
  303.7 8.7 %convolution_convert_fusion.1 = bf16[1024,2048]{1,0:T(8,128)(2,1)} fusion(bf16[1536,1024]{1,0:T(8,128)(2,1)S(1)} %get-tuple-element.21, bf16[1536,2048]{1,0:T(8,128)(2,1)S(1)} %bitcast.191), kind=kOutput, calls=%fused_computation.16 | convolution fusion | flops 6444548096 | bytes 13631488 | tf_op jit(solution)/shard_map/dot_general | solution.py:24
  312.3 14.2 %fusion.6 = bf16[1536,1024]{1,0:T(8,128)(2,1)S(1)} fusion(f32[1536,1024]{1,0:T(8,128)} %get-tuple-element.55, bf16[1536,2048]{1,0:T(8,128)(2,1)} %constant_dynamic-update-slice_fusion.5, bf16[1024,2048]{1,0:T(8,128)(2,1)} %bitcast.159), kind=kOutput, calls=%fused_computation.8 | convolution fusion | flops 6473908224 | bytes 19922944 | tf_op jit(solution)/shard_map/dot_general | solution.py:30
  345.7 18.9 %collective-permute-done.17 = bf16[384,2048]{1,0:T(8,128)(2,1)S(1)} collective-permute-done((bf16[384,2048]{1,0:T(8,128)(2,1)S(1)}, bf16[384,2048]{1,0:T(8,128)(2,1)S(1)}, u32[]{:S(2)}, u32[]{:S(2)}) %collective-permute-start.17) | collective-permute-done | bytes 1572896 | tf_op jit(solution)/shard_map/ppermute | solution.py:61
  369.2 8.5 %convolution_convert_fusion = bf16[2048,1024]{1,0:T(8,128)(2,1)} fusion(bf16[1536,2048]{1,0:T(8,128)(2,1)S(1)} %bitcast.193, bf16[1536,1024]{1,0:T(8,128)(2,1)S(1)} %fusion.6), kind=kOutput, calls=%fused_computation.15 | convolution fusion | flops 6444548096 | bytes 13631488 | tf_op jit(solution)/shard_map/dot_general | solution.py:24
  387.7 10.7 %collective-permute-done.19 = bf16[192,2048]{1,0:T(8,128)(2,1)S(1)} collective-permute-done((bf16[192,2048]{1,0:T(8,128)(2,1)}, bf16[192,2048]{1,0:T(8,128)(2,1)S(1)}, u32[]{:S(2)}, u32[]{:S(2)}) %collective-permute-start.19) | collective-permute-done | bytes 786464 | tf_op jit(solution)/shard_map/ppermute | solution.py:57
  401.1 18.9 %collective-permute-done.20 = bf16[384,2048]{1,0:T(8,128)(2,1)S(1)} collective-permute-done((bf16[384,2048]{1,0:T(8,128)(2,1)S(1)}, bf16[384,2048]{1,0:T(8,128)(2,1)S(1)}, u32[]{:S(2)}, u32[]{:S(2)}) %collective-permute-start.20) | collective-permute-done | bytes 1572896 | tf_op jit(solution)/shard_map/ppermute | solution.py:61
  430.4 12.5 %attend_back.1 = bf16[1536,768]{1,0:T(8,128)(2,1)} custom-call(s32[8]{0:T(128)} %convert_add_fusion.5.item_lengths, bf16[1536,768]{1,0:T(8,128)(2,1)} %convolution_convert_fusion.6.qkv, bf16[1536,256]{1,0:T(8,128)(2,1)} %convolution_convert_fusion.9.grad_mixed), custom_call_target="tpu_custom_call" | custom-call | flops 905969664 | bytes 5505024 | tf_op jit(solution)/shard_map/attend_back/pallas_call | solution.py:165
  449.3 9.7 %convolution_convert_fusion.7 = bf16[2048,768]{0,1:T(8,128)(2,1)} fusion(bf16[1536,2048]{1,0:T(8,128)(2,1)} %constant_dynamic-update-slice_fusion, bf16[1536,768]{1,0:T(8,128)(2,1)S(1)} %copy-done.19), kind=kOutput, calls=%fused_computation.22 | convolution fusion | flops 4833411072 | bytes 11796480 | tf_op jit(solution)/shard_map/dot_general | solution.py:24
  499.0 8.1 %collective-permute-done.27 = bf16[384,2048]{1,0:T(8,128)(2,1)} collective-permute-done((bf16[384,2048]{1,0:T(8,128)(2,1)}, bf16[384,2048]{1,0:T(8,128)(2,1)}, u32[]{:S(2)}, u32[]{:S(2)}) %collective-permute-start.27) | collective-permute-done | bytes 1572896 | tf_op jit(solution)/shard_map/ppermute | solution.py:61
  515.3 19.4 %reduce-scatter.8.cloned.1.call-done = bf16[256,2048]{1,0:T(8,128)(2,1)} async-done(((bf16[1024,2048]{1,0:T(8,128)(2,1)}), bf16[256,2048]{1,0:T(8,128)(2,1)}) %reduce-scatter.8.cloned.1.call-update) | async-done | bytes 1048592 | tf_op jit(solution)/shard_map/reduce_scatter | solution.py:115
  561.4 53.0 %reduce-scatter.4.cloned.1.call-done = bf16[512,1024]{0,1:T(8,128)(2,1)} async-done(((bf16[2048,1024]{0,1:T(8,128)(2,1)}), bf16[512,1024]{0,1:T(8,128)(2,1)}) %reduce-scatter.4.cloned.1.call-update) | async-done | bytes 1048592 | tf_op jit(solution)/shard_map/reduce_scatter | solution.py:115
  (304 shorter events, 265.6 us)
Async XLA Ops:
  17.1 105.3 %all-gather.3.cloned.1.call-start = ((), (), s32[]{:S(2)}) async-start(), calls=%async_computation.9 | async-start | bytes 5242880 | tf_op jit(solution)/shard_map/all_gather | solution.py:111
  50.9 27.7 %collective-permute-start.5 = (bf16[384,2048]{1,0:T(8,128)(2,1)}, bf16[384,2048]{1,0:T(8,128)(2,1)}, u32[]{:S(2)}, u32[]{:S(2)}) collective-permute-start(bf16[384,2048]{1,0:T(8,128)(2,1)} %pad_maximum_fusion.3), channel_id=1, source_target_pairs={{0,4},{1,3},{2,6},{3,1},{4,0},{5,7},{6,2},{7,5},{8,12},{9,11},{10,... | collective-permute-start | bytes 4718600 | tf_op jit(solution)/shard_map/ppermute | solution.py:61
  64.0 32.8 %collective-permute-start.1 = (bf16[384,2048]{1,0:T(8,128)(2,1)}, bf16[384,2048]{1,0:T(8,128)(2,1)}, u32[]{:S(2)}, u32[]{:S(2)}) collective-permute-start(bf16[384,2048]{1,0:T(8,128)(2,1)} %pad_maximum_fusion.2), channel_id=1, source_target_pairs={{0,4},{1,3},{2,6},{3,1},{4,0},{5,7},{6,2},{7,5},{8,12},{9,11},{10,... | collective-permute-start | bytes 4718600 | tf_op jit(solution)/shard_map/ppermute | solution.py:61
  68.3 35.8 %all-to-all-start.1 = ((bf16[8,64,1024]{2,1,0:T(8,128)(2,1)}), bf16[8,64,1024]{2,1,0:T(8,128)(2,1)S(1)}, u32[]{:S(2)}, u32[]{:S(2)}) async-start(bf16[8,64,1024]{2,1,0:T(8,128)(2,1)} %reshape.236), calls=%async_computation.1 | async-start | bytes 2097152 | tf_op jit(solution)/shard_map/all_to_all | solution.py:213
  72.0 189.4 %all-gather.5.cloned.1.call-start = ((), (), s32[]{:S(2)}) async-start(), calls=%async_computation.10 | async-start | bytes 10485760 | tf_op jit(solution)/shard_map/all_gather | solution.py:111
  74.9 33.6 %collective-permute-start.6 = (bf16[384,2048]{1,0:T(8,128)(2,1)}, bf16[384,2048]{1,0:T(8,128)(2,1)}, u32[]{:S(2)}, u32[]{:S(2)}) collective-permute-start(bf16[384,2048]{1,0:T(8,128)(2,1)} %pad_maximum_fusion.3), channel_id=1, source_target_pairs={{0,1},{1,0},{2,3},{3,2},{4,5},{5,4},{6,7},{7,6},{8,9},{9,8},{10,11... | collective-permute-start | bytes 4718600 | tf_op jit(solution)/shard_map/ppermute | solution.py:65
  75.7 38.2 %collective-permute-start.2 = (bf16[384,2048]{1,0:T(8,128)(2,1)}, bf16[384,2048]{1,0:T(8,128)(2,1)}, u32[]{:S(2)}, u32[]{:S(2)}) collective-permute-start(bf16[384,2048]{1,0:T(8,128)(2,1)} %pad_maximum_fusion.2), channel_id=1, source_target_pairs={{0,1},{1,0},{2,3},{3,2},{4,5},{5,4},{6,7},{7,6},{8,9},{9,8},{10,11... | collective-permute-start | bytes 4718600 | tf_op jit(solution)/shard_map/ppermute | solution.py:65
  78.6 38.1 %collective-permute-start.7 = (bf16[384,2048]{1,0:T(8,128)(2,1)}, bf16[384,2048]{1,0:T(8,128)(2,1)}, u32[]{:S(2)}, u32[]{:S(2)}) collective-permute-start(bf16[384,2048]{1,0:T(8,128)(2,1)} %collective-permute-done.5), channel_id=1, source_target_pairs={{0,1},{1,0},{2,3},{3,2},{4,5},{5,4},{6,7},{7,6},{8,9},{9,8},{10,11... | collective-permute-start | bytes 4718600 | tf_op jit(solution)/shard_map/ppermute | solution.py:65
  96.8 22.7 %collective-permute-start.3 = (bf16[384,2048]{1,0:T(8,128)(2,1)}, bf16[384,2048]{1,0:T(8,128)(2,1)}, u32[]{:S(2)}, u32[]{:S(2)}) collective-permute-start(bf16[384,2048]{1,0:T(8,128)(2,1)} %collective-permute-done.1), channel_id=1, source_target_pairs={{0,1},{1,0},{2,3},{3,2},{4,5},{5,4},{6,7},{7,6},{8,9},{9,8},{10,11... | collective-permute-start | bytes 4718600 | tf_op jit(solution)/shard_map/ppermute | solution.py:65
  105.6 389.5 %reduce-scatter.6.cloned.1.call-start = ((), (), s32[]{:S(2)}) async-start(), calls=%async_computation.12 | async-start | bytes 5242880 | tf_op jit(solution)/shard_map/reduce_scatter | solution.py:115
  154.7 20.5 %collective-permute-start.10 = (bf16[384,2048]{1,0:T(8,128)(2,1)S(1)}, bf16[384,2048]{1,0:T(8,128)(2,1)S(1)}, u32[]{:S(2)}, u32[]{:S(2)}) collective-permute-start(bf16[384,2048]{1,0:T(8,128)(2,1)S(1)} %slice.330), channel_id=1, source_target_pairs={{0,4},{1,3},{2,6},{3,1},{4,0},{5,7},{6,2},{7,5},{8,12},{9,11},{10,... | collective-permute-start | bytes 4718600 | tf_op jit(solution)/shard_map/ppermute | solution.py:61
  206.5 20.7 %collective-permute-start.13 = (bf16[384,2048]{1,0:T(8,128)(2,1)}, bf16[384,2048]{1,0:T(8,128)(2,1)}, u32[]{:S(2)}, u32[]{:S(2)}) collective-permute-start(bf16[384,2048]{1,0:T(8,128)(2,1)} %pad_maximum_fusion.4), channel_id=1, source_target_pairs={{0,4},{1,3},{2,6},{3,1},{4,0},{5,7},{6,2},{7,5},{8,12},{9,11},{10,... | collective-permute-start | bytes 4718600 | tf_op jit(solution)/shard_map/ppermute | solution.py:61
  207.0 77.7 %collective-permute-start.14 = (bf16[384,2048]{1,0:T(8,128)(2,1)}, bf16[384,2048]{1,0:T(8,128)(2,1)}, u32[]{:S(2)}, u32[]{:S(2)}) collective-permute-start(bf16[384,2048]{1,0:T(8,128)(2,1)} %pad_maximum_fusion.4), channel_id=1, source_target_pairs={{0,1},{1,0},{2,3},{3,2},{4,5},{5,4},{6,7},{7,6},{8,9},{9,8},{10,11... | collective-permute-start | bytes 4718600 | tf_op jit(solution)/shard_map/ppermute | solution.py:65
  227.2 60.1 %collective-permute-start.15 = (bf16[384,2048]{1,0:T(8,128)(2,1)}, bf16[384,2048]{1,0:T(8,128)(2,1)}, u32[]{:S(2)}, u32[]{:S(2)}) collective-permute-start(bf16[384,2048]{1,0:T(8,128)(2,1)} %collective-permute-done.13), channel_id=1, source_target_pairs={{0,1},{1,0},{2,3},{3,2},{4,5},{5,4},{6,7},{7,6},{8,9},{9,8},{10,11... | collective-permute-start | bytes 4718600 | tf_op jit(solution)/shard_map/ppermute | solution.py:65
  344.1 20.5 %collective-permute-start.17 = (bf16[384,2048]{1,0:T(8,128)(2,1)S(1)}, bf16[384,2048]{1,0:T(8,128)(2,1)S(1)}, u32[]{:S(2)}, u32[]{:S(2)}) collective-permute-start(bf16[384,2048]{1,0:T(8,128)(2,1)S(1)} %slice.329), channel_id=1, source_target_pairs={{0,4},{1,3},{2,6},{3,1},{4,0},{5,7},{6,2},{7,5},{8,12},{9,11},{10,... | collective-permute-start | bytes 4718600 | tf_op jit(solution)/shard_map/ppermute | solution.py:61
  380.0 154.6 %reduce-scatter.8.cloned.1.call-start = ((), (), s32[]{:S(2)}) async-start(), calls=%async_computation.13 | async-start | bytes 5242880 | tf_op jit(solution)/shard_map/reduce_scatter | solution.py:115
  387.6 226.8 %reduce-scatter.4.cloned.1.call-start = ((), (), s32[]{:S(2)}) async-start(), calls=%async_computation.11 | async-start | bytes 5242880 | tf_op jit(solution)/shard_map/reduce_scatter | solution.py:115
  401.1 21.2 %collective-permute-start.21 = (bf16[384,2048]{1,0:T(8,128)(2,1)S(1)}, bf16[384,2048]{1,0:T(8,128)(2,1)S(1)}, u32[]{:S(2)}, u32[]{:S(2)}) collective-permute-start(bf16[384,2048]{1,0:T(8,128)(2,1)S(1)} %pad_maximum_fusion.5), channel_id=1, source_target_pairs={{0,1},{1,0},{2,3},{3,2},{4,5},{5,4},{6,7},{7,6},{8,9},{9,8},{10,11... | collective-permute-start | bytes 4718600 | tf_op jit(solution)/shard_map/ppermute | solution.py:65
  483.3 23.8 %collective-permute-start.27 = (bf16[384,2048]{1,0:T(8,128)(2,1)}, bf16[384,2048]{1,0:T(8,128)(2,1)}, u32[]{:S(2)}, u32[]{:S(2)}) collective-permute-start(bf16[384,2048]{1,0:T(8,128)(2,1)} %slice.327), channel_id=1, source_target_pairs={{0,4},{1,3},{2,6},{3,1},{4,0},{5,7},{6,2},{7,5},{8,12},{9,11},{10,... | collective-permute-start | bytes 4718600 | tf_op jit(solution)/shard_map/ppermute | solution.py:61
  493.6 43.8 %collective-permute-start.24 = (bf16[384,2048]{1,0:T(8,128)(2,1)}, bf16[384,2048]{1,0:T(8,128)(2,1)}, u32[]{:S(2)}, u32[]{:S(2)}) collective-permute-start(bf16[384,2048]{1,0:T(8,128)(2,1)} %slice.328), channel_id=1, source_target_pairs={{0,4},{1,3},{2,6},{3,1},{4,0},{5,7},{6,2},{7,5},{8,12},{9,11},{10,... | collective-permute-start | bytes 4718600 | tf_op jit(solution)/shard_map/ppermute | solution.py:61
  495.2 49.3 %all-to-all-start.5 = ((bf16[8,64,1024]{2,1,0:T(8,128)(2,1)}), bf16[8,64,1024]{2,1,0:T(8,128)(2,1)S(1)}, u32[]{:S(2)}, u32[]{:S(2)}) async-start(bf16[8,64,1024]{2,1,0:T(8,128)(2,1)} %bitcast.181), calls=%async_computation.7 | async-start | bytes 2097152 | tf_op jit(solution)/shard_map/all_to_all | solution.py:319
  512.7 39.0 %collective-permute-start.28 = (bf16[192,2048]{1,0:T(8,128)(2,1)}, bf16[192,2048]{1,0:T(8,128)(2,1)S(1)}, u32[]{:S(2)}, u32[]{:S(2)}) collective-permute-start(bf16[192,2048]{1,0:T(8,128)(2,1)} %slice.331), channel_id=1, source_target_pairs={{0,2},{1,5},{2,0},{3,7},{4,6},{5,1},{6,4},{7,3},{8,10},{9,13},{10,... | collective-permute-start | bytes 2359304 | tf_op jit(solution)/shard_map/ppermute | solution.py:57
  543.0 77.5 %collective-permute-start.25 = (bf16[192,2048]{1,0:T(8,128)(2,1)}, bf16[192,2048]{1,0:T(8,128)(2,1)}, u32[]{:S(2)}, u32[]{:S(2)}) collective-permute-start(bf16[192,2048]{1,0:T(8,128)(2,1)} %slice.332), channel_id=1, source_target_pairs={{0,2},{1,5},{2,0},{3,7},{4,6},{5,1},{6,4},{7,3},{8,10},{9,13},{10,... | collective-permute-start | bytes 2359304 | tf_op jit(solution)/shard_map/ppermute | solution.py:57
  553.4 63.4 %all-to-all-start.3 = ((f32[32,1,128]{2,1,0:T(1,128)}), f32[32,1,128]{2,1,0:T(1,128)S(1)}, u32[]{:S(2)}, u32[]{:S(2)}) async-start(f32[32,1,128]{2,1,0:T(1,128)} %reshape.287), calls=%async_computation.3 | async-start | bytes 32768 | tf_op jit(solution)/shard_map/all_to_all | solution.py:312
  (63 other events, 654.7 us)
Sparse Core Ops, SparseCore 0:
  31.0 80.0 all-gather.2
  113.3 148.0 all-gather.4
  380.2 74.9 reduce-scatter.5
  457.3 77.2 reduce-scatter.7
  536.8 77.5 reduce-scatter.3

commit v3 on v2

--- a/solution.py
+++ b/solution.py
@@ -1,3 +1,5 @@
+import math
+
 import jax
 import jax.numpy as jnp
 from jax import lax
@@ -33,7 +35,8 @@
 
 
 def gelu_tanh(values):
-    return jax.nn.gelu(values, approximate=True)
+    inner = (2.0 / math.pi) ** 0.5 * (values + 0.044715 * values * values * values)
+    return 0.5 * values * (1.0 + jnp.tanh(inner))
 
 
 def norm_stats(values):
@@ -75,25 +78,24 @@
         near = after(near, *others)
     pair = jnp.concatenate([block, near], axis=0)
     other = second_hop(pair)
-    return jnp.concatenate([pair, other, core_hop(pair), core_hop(other)], axis=0)
-
-
-def team_sum(terms_of, rows, held=None, beside=None):
+    return pair, other, core_hop(pair), core_hop(other)
+
+
+def join(blocks):
+    return jnp.concatenate(blocks, axis=0)
+
+
+def team_sum(terms_of, rows, held=None):
     low = jnp.bfloat16
     half = rows.shape[0] // 2
     quarter = half // 2
     arrived = core_hop(terms_of(rows[half:]).astype(low))
     near = terms_of(rows[:half]) + arrived.astype(jnp.float32)
-    if beside is not None:
-        held = after(held, arrived)
     far = second_hop(near[quarter:].astype(low))
     near = near[:quarter] + far.astype(jnp.float32)
     last = first_hop(near[quarter // 2 :].astype(low))
-    if beside is None:
-        return near[: quarter // 2] + last.astype(jnp.float32)
-    result = beside(held)
-    last, result = lax.optimization_barrier((last, result))
-    return near[: quarter // 2] + last.astype(jnp.float32), result
+    total = near[: quarter // 2] + last.astype(jnp.float32)
+    return total if held is None else (total, after(held, arrived))
 
 
 def meet(kept, sent):
@@ -152,6 +154,77 @@
         grad_qkv[:, at : at + HD] = (gram_rows(grad_scores, queries) * score_scale).astype(low)
         at += width
         grad_qkv[:, at : at + HD] = gram_rows(probs.astype(low), grad_own).astype(low)
+
+
+def mlp_kernel(*refs):
+    *parts, grad_low, w_up, w_down, active, grad_hidden, terms, normed = refs
+    step = pl.program_id(0)
+    blocks, strips, units, columns = w_down.shape
+    width = w_up.shape[3]
+    low = active.dtype
+
+    @pl.when(step == 0)
+    def _():
+        rows = parts[0].shape[0]
+        for at, part in enumerate(parts):
+            normed[at * rows : (at + 1) * rows] = part[...]
+
+    hidden = matmul(normed[...], w_up[...].reshape(-1, width))
+    value, back = jax.vjp(gelu_tanh, hidden)
+    own = value.astype(low)
+    active[...] = own
+    grad_active = 0.0
+    for s in range(strips):
+        part = w_down[:, s].reshape(width, columns)
+        grad_active += times_transposed(grad_low[:, s * columns : (s + 1) * columns], part)
+    own_grad = back(grad_active)[0].astype(low)
+    grad_hidden[...] = own_grad
+    for s in range(strips):
+        part = gram_rows(own, grad_low[:, s * columns : (s + 1) * columns]).astype(low)
+        terms[pl.ds(step * blocks, blocks), s, :, columns:] = part.reshape(blocks, units, columns)
+    part = gram_rows(normed[...], own_grad).astype(low)
+    at = pl.multiple_of(step * width, width)
+    terms[:, :, :, pl.ds(at, width)] = part.reshape(terms.shape[:3] + (width,))
+
+
+def mlp_call(parts, grad_low, weights):
+    rows, features = grad_low.shape
+    layers, strips, units, columns = weights.shape
+    own_units = columns // 2
+    blocks = max(1, 256 // units)
+    width = blocks * units
+    low = grad_low.dtype
+
+    def whole(shape):
+        return pl.BlockSpec(shape, lambda step: (0,) * len(shape), pipeline_mode=pl.Buffered(1))
+
+    return pl.pallas_call(
+        mlp_kernel,
+        out_shape=(
+            jax.ShapeDtypeStruct((rows, own_units), low),
+            jax.ShapeDtypeStruct((rows, own_units), low),
+            jax.ShapeDtypeStruct(weights.shape, low),
+        ),
+        grid=(own_units // width,),
+        in_specs=[whole(part.shape) for part in parts]
+        + [
+            whole((rows, features)),
+            pl.BlockSpec((layers, strips, units, width), lambda step: (0, 0, 0, step)),
+            pl.BlockSpec((blocks, strips, units, own_units), lambda step: (step, 0, 0, 1)),
+        ],
+        out_specs=(
+            pl.BlockSpec((rows, width), lambda step: (0, step)),
+            pl.BlockSpec((rows, width), lambda step: (0, step)),
+            whole(weights.shape),
+        ),
+        scratch_shapes=[pltpu.VMEM((rows, features), low)],
+        cost_estimate=pl.CostEstimate(
+            flops=8 * rows * features * own_units,
+            bytes_accessed=4 * rows * (features + own_units) + 8 * features * own_units,
+            transcendentals=rows * own_units,
+        ),
+        name="mlp",
+    )(*parts, grad_low, weights, weights)
 
 
 def attend_call(kernel, name, slots, lengths, operands, width, products):
@@ -206,9 +279,8 @@
 
     qkv_cut = jnp.concatenate([own_columns(w_query), own_columns(w_key), own_columns(w_value)], axis=2)
     qkv_cut = lax.all_to_all(qkv_cut, TEAM, 0, 0, tiled=True).reshape(team * depth, 3 * own_width)
-    strip = features // team
-    out_cut = w_out.reshape(depth, team, strip).transpose(1, 0, 2).reshape(team * depth, strip)
-    w_attn = weight_gather(jnp.concatenate([qkv_cut, out_cut], axis=1))
+    out_rows = weight_gather(w_out)
+    w_qkv = weight_gather(qkv_cut)
     up_cut = w_up.reshape(depth, layers, team, units).transpose(2, 0, 1, 3)
     up_cut = lax.all_to_all(up_cut.reshape(team, depth, own_units), TEAM, 0, 0, tiled=True)
     up_cut = up_cut.reshape(team * depth, own_units)
@@ -240,12 +312,11 @@
     cotangent_low = jnp.where(live, cotangent.reshape(row_count, features), jnp.zeros((), low))
     grad_stream = cotangent_low.astype(jnp.float32)
     grad_low = team_gather(cotangent_low)
-    normed_a = after(normed_a, up_cut, grad_low)
-
-    w_qkv = w_attn[:, : 3 * own_width]
+    normed_a = join(after(normed_a, up_cut, grad_low))
+    grad_low = join(grad_low)
+
     qkv = matmul(normed_a, w_qkv).astype(low)
-    out_rows = w_attn[:, 3 * own_width :].reshape(layers, team, depth, strip)
-    out_rows = out_rows.transpose(0, 2, 1, 3).reshape(layers, depth, features)
+    out_rows = out_rows.reshape(layers, depth, features)
     if head_parts == 2:
         w_out_own = meet(*own_part(out_rows.reshape(2, own_heads, depth, features)))
     else:
@@ -257,29 +328,21 @@
 
     scaled_m, inverse_m = norm_stats(residual)
     normed_m = team_gather((scaled_m * full_gain_m).astype(low))
+    normed_m, w_mlp = lax.optimization_barrier((normed_m, w_mlp))
     w_up_own = w_mlp[:, :own_units]
-    w_down_own = w_mlp[:, own_units:].reshape(layers, strips, units, own_units)
-    w_down_own = w_down_own.transpose(0, 2, 1, 3).reshape(own_units, features)
-    hidden = matmul(normed_m, w_up_own)
-    gelu_value, gelu_back = jax.vjp(gelu_tanh, hidden)
-    active = gelu_value.astype(low)
-
-    grad_down = gram_rows(active, grad_low).astype(low)
-    grad_down, grad_low = lax.optimization_barrier((grad_down, grad_low))
-    grad_down = weight_scatter(grad_down)
-    grad_active = times_transposed(grad_low, w_down_own)
-    grad_hidden = gelu_back(grad_active)[0].astype(low)
-    grad_normed_m, grad_up = team_sum(
-        lambda rows: times_transposed(rows, w_up_own),
-        grad_hidden,
-        grad_hidden,
-        lambda held: gram_rows(normed_m, held).astype(low),
-    )
-    grad_up = weight_scatter(grad_up)
+
+    weights = w_mlp.reshape(layers, strips, units, 2 * own_units)
+    active, grad_hidden, grad_mlp = mlp_call(normed_m, grad_low, weights)
+    grad_mlp = weight_scatter(grad_mlp.reshape(features, 2 * own_units))
+    w_down_own = jnp.concatenate(
+        [weights[:, s, :, own_units:].reshape(own_units, own_units) for s in range(strips)], axis=1
+    )
+    w_down_own = lax.optimization_barrier(w_down_own)
+    grad_normed_m = team_sum(lambda rows: times_transposed(rows, w_up_own), grad_hidden)
     gain_m_terms = jnp.sum(grad_normed_m * scaled_m, axis=0)
     grad_residual = norm_backward(grad_normed_m * full_gain_m, scaled_m, inverse_m) + grad_stream
 
-    grad_residual_low = team_gather(grad_residual.astype(low))
+    grad_residual_low = join(team_gather(grad_residual.astype(low)))
     grad_mixed = times_transposed(grad_residual_low, w_out_own).astype(low)
     grad_qkv = attend_call(
         attend_back_kernel, "attend_back", slot_count, team_lengths, (qkv, grad_mixed), 3 * own_width, 6
@@ -295,15 +358,17 @@
         )
     else:
         grad_out = lax.all_to_all(grad_out, head_axes, 0, 0, tiled=True)
+    strip = features // team
     grad_out = grad_out.reshape(layers, depth, team, strip).transpose(0, 2, 1, 3)
     grad_out = grad_out.reshape(features, strip)
     grad_qkv_w = gram_rows(normed_a, grad_qkv).astype(low)
-    grad_attn = weight_scatter(jnp.concatenate([grad_qkv_w, grad_out], axis=1))
+    grad_attn = jnp.concatenate([grad_qkv_w, grad_out], axis=1)
+    grad_qkv, grad_attn = lax.optimization_barrier((grad_qkv, grad_attn))
+    grad_attn = weight_scatter(grad_attn)
     grad_qkv_w = grad_attn[:, : 3 * own_width]
     grad_out = grad_attn[:, 3 * own_width :].reshape(team, depth, strip)
     grad_out = grad_out.transpose(1, 0, 2).reshape(depth, features)
-    grad_normed_a = team_sum(lambda rows: times_transposed(rows, w_qkv), grad_qkv)
-    active = after(active, grad_qkv)
+    grad_normed_a, active = team_sum(lambda rows: times_transposed(rows, w_qkv), grad_qkv, active)
     output = residual + team_sum(lambda rows: matmul(rows, w_down_own), active)
     gain_a_terms = jnp.sum(grad_normed_a * scaled_a, axis=0)
     grad_input = norm_backward(grad_normed_a * full_gain_a, scaled_a, inverse_a) + grad_residual
@@ -316,6 +381,10 @@
         cut = cut.reshape(head_groups, head_parts, depth, own_heads, HD)
         return cut.transpose(2, 1, 3, 0, 4).reshape(depth, features).astype(jnp.float32)
 
+    grad_up = grad_mlp[:, :own_units]
+    grad_down = jnp.concatenate(
+        [grad_mlp[s * units : (s + 1) * units, own_units:] for s in range(strips)], axis=1
+    )
     grad_up = lax.all_to_all(grad_up.reshape(team, depth, own_units), TEAM, 0, 0, tiled=True)
     grad_up = grad_up.reshape(team, depth, layers, units).transpose(1, 2, 0, 3)
     grad_up = grad_up.reshape(depth, layers * team * units).astype(jnp.float32)

time: 654 us -> 568 us (0.87)
  matrix products: 104 us -> 59.6 us
  Pallas kernels: 22.3 us -> 62.5 us
  local copies, waits for them, and re-layouts: 107 us -> 67 us
  waiting for transfers between devices: 298 us -> 266 us
    reduce_scatter x3 -> x2, waiting for transfers between devices: 72.4 us -> 0.01 us  [weight_scatter(): lax.psum_scatter(terms.astype(jnp.bfloat16), 'z', scatter_dimension=0, ti...]
    pallas_call x0 -> x1, Pallas kernels: none -> 40.4 us  [mlp_call(): pl.pallas_call(mlp_kernel, out_shape=(jax.ShapeDtypeStruct((rows, own_uni...]
    unnamed x112 -> x78, local copies, waits for them, and re-layouts: 52.4 us -> 26.4 us
    dot_general x4 -> x2, matrix products: 31.6 us -> 10.9 us  [gram_rows(): lax.dot_general(left_side, right_side, (((0,), (0,)), ((), ())), preferre...]
    ppermute x8, waiting for transfers between devices: 49.7 us -> 63.5 us  [first_hop(): return lax.ppermute(block, TEAM, [(t, t ^ FIRST[t & 1]) for t in range(8)])]
    ppermute x8, waiting for transfers between devices: 102 us -> 115 us  [second_hop(): return lax.ppermute(block, TEAM, [(t, t ^ SECOND[t & 1]) for t in range(8)])]
    dot_general x6 -> x5, matrix products: 32.7 us -> 19.9 us  [matmul(): return jnp.dot(left_side, right_side, preferred_element_type=jnp.float32)]
    dot_general x6 -> x5, matrix products: 40.1 us -> 28.8 us  [times_transposed(): lax.dot_general(left_side, right_side, (((1,), (1,)), ((), ())), preferre...]
  transfers between devices with their start and end apart: 41 -> 41, of which waited for: 21 -> 23; matrix products, arithmetic and copies ran while one was open for 28% -> 26% of each run, Pallas kernels for 3% -> 4%
where the time goes in v3:
time: 568 us; the launch traced here: 561 us
  waiting for transfers between devices  266 us (47%)
  local copies, waits for them, and re-layouts  67 us (12%)
  Pallas kernels  62.5 us (11%)
  matrix products  59.6 us (10%)
  starting transfers between devices  48.6 us (9%)
  other arithmetic  41.6 us (7%)
  between operations  15.6 us (3%)
    ppermute x8, waiting for transfers between devices, second_hop(): return lax.ppermute(block, TEAM, [(t, t ^ SECOND[t & 1]) for t in range(8)])  115 us
    ppermute x8, waiting for transfers between devices, first_hop(): return lax.ppermute(block, TEAM, [(t, t ^ FIRST[t & 1]) for t in range(8)])  63.5 us
    pallas_call x1, Pallas kernels, mlp_call(): pl.pallas_call(mlp_kernel, out_shape=(jax.ShapeDtypeStruct((rows, own_uni...  40.4 us
    all_gather x3, waiting for transfers between devices, weight_gather(): return lax.all_gather(block, 'z', axis=0, tiled=True)  32.8 us
    dot_general x5, matrix products, times_transposed(): lax.dot_general(left_side, right_side, (((1,), (1,)), ((), ())), preferre...  28.8 us
    unnamed x78, local copies, waits for them, and re-layouts  26.4 us
    pallas_call x2, Pallas kernels, attend_call(): pl.pallas_call(kernel, out_shape=jax.ShapeDtypeStruct((rows, width), oper...  22.1 us
    dot_general x5, matrix products, matmul(): return jnp.dot(left_side, right_side, preferred_element_type=jnp.float32)  19.9 us
  transfers between devices with their start and end apart: 41, of which 23 were waited for; matrix products, arithmetic and copies ran while one was open for 26% of the time, Pallas kernels for 4%

profile of v3, /device:TPU:0, one launch (start us, length us, event | category | flops | bytes accessed | tf_op | source)
XLA Modules:
  0.0 561.2 jit_solution(4966822439561383390)
XLA Ops:
  22.0 8.5 %all-to-all-done.2 = bf16[8,64,768]{2,1,0:T(8,128)(2,1)S(1)} async-done(((bf16[8,64,768]{2,1,0:T(8,128)(2,1)}), bf16[8,64,768]{2,1,0:T(8,128)(2,1)S(1)}, u32[]{:S(2)}, u32[]{:S(2)}) %all-to-all-start.2) | async-done | bytes 786464 | tf_op jit(solution)/shard_map/all_to_all | solution.py:281
  36.2 6.6 %all-to-all-done = bf16[32,3,64]{2,1,0:T(4,128)(2,1)S(1)} async-done(((bf16[32,3,64]{2,1,0:T(4,128)(2,1)}), bf16[32,3,64]{2,1,0:T(4,128)(2,1)S(1)}, u32[]{:S(2)}, u32[]{:S(2)}) %all-to-all-start) | async-done | bytes 12320 | tf_op jit(solution)/shard_map/all_to_all | solution.py:295
  46.2 16.6 %collective-permute-done = bf16[192,2048]{1,0:T(8,128)(2,1)S(1)} collective-permute-done((bf16[192,2048]{1,0:T(8,128)(2,1)S(1)}, bf16[192,2048]{1,0:T(8,128)(2,1)S(1)}, u32[]{:S(2)}, u32[]{:S(2)}) %collective-permute-start) | collective-permute-done | bytes 786464 | tf_op jit(solution)/shard_map/ppermute | solution.py:60
  73.9 20.1 %collective-permute-done.1 = bf16[384,2048]{1,0:T(8,128)(2,1)} collective-permute-done((bf16[384,2048]{1,0:T(8,128)(2,1)S(1)}, bf16[384,2048]{1,0:T(8,128)(2,1)}, u32[]{:S(2)}, u32[]{:S(2)}) %collective-permute-start.1) | collective-permute-done | bytes 1572896 | tf_op jit(solution)/shard_map/ppermute | solution.py:64
  115.6 9.6 %convolution_convert_fusion.3.qkv = bf16[1536,768]{1,0:T(8,128)(2,1)} fusion(bf16[1536,2048]{1,0:T(8,128)(2,1)} %constant_dynamic-update-slice_fusion, bf16[2048,768]{1,0:T(8,128)(2,1)} %all-gather.4.cloned.1.call-done), kind=kOutput, calls=%fused_computation.14 | convolution fusion | flops 4833017856 | bytes 11796480 | tf_op jit(solution)/shard_map/dot_general | solution.py:22
  125.3 9.6 %attend.1 = bf16[1536,256]{1,0:T(8,128)(2,1)} custom-call(s32[8]{0:T(128)} %convert_add_fusion.5.item_lengths, bf16[1536,768]{1,0:T(8,128)(2,1)} %convolution_convert_fusion.3.qkv), custom_call_target="tpu_custom_call" | custom-call | flops 301989888 | bytes 3145728 | tf_op jit(solution)/shard_map/attend/pallas_call | solution.py:238
  145.4 19.0 %collective-permute-done.10 = bf16[384,2048]{1,0:T(8,128)(2,1)S(1)} collective-permute-done((bf16[384,2048]{1,0:T(8,128)(2,1)S(1)}, bf16[384,2048]{1,0:T(8,128)(2,1)S(1)}, u32[]{:S(2)}, u32[]{:S(2)}) %collective-permute-start.10) | collective-permute-done | bytes 1572896 | tf_op jit(solution)/shard_map/ppermute | solution.py:64
  167.3 11.6 %collective-permute-done.11 = bf16[192,2048]{1,0:T(8,128)(2,1)} collective-permute-done((bf16[192,2048]{1,0:T(8,128)(2,1)S(1)}, bf16[192,2048]{1,0:T(8,128)(2,1)}, u32[]{:S(2)}, u32[]{:S(2)}) %collective-permute-start.11) | collective-permute-done | bytes 786464 | tf_op jit(solution)/shard_map/ppermute | solution.py:60
  182.0 11.6 %collective-permute-done.12 = bf16[192,2048]{1,0:T(8,128)(2,1)S(1)} collective-permute-done((bf16[192,2048]{1,0:T(8,128)(2,1)S(1)}, bf16[192,2048]{1,0:T(8,128)(2,1)S(1)}, u32[]{:S(2)}, u32[]{:S(2)}) %collective-permute-start.12) | collective-permute-done | bytes 786464 | tf_op jit(solution)/shard_map/ppermute | solution.py:60
  195.3 19.1 %collective-permute-done.13.refs_1_ = bf16[384,2048]{1,0:T(8,128)(2,1)} collective-permute-done((bf16[384,2048]{1,0:T(8,128)(2,1)S(1)}, bf16[384,2048]{1,0:T(8,128)(2,1)}, u32[]{:S(2)}, u32[]{:S(2)}) %collective-permute-start.13) | collective-permute-done | bytes 1572896 | tf_op jit(solution)/shard_map/ppermute | solution.py:64
  223.6 32.8 %all-gather.8.cloned.1.call-done = bf16[2048,2048]{1,0:T(8,128)(2,1)} async-done(((bf16[512,2048]{1,0:T(8,128)(2,1)}), bf16[2048,2048]{1,0:T(8,128)(2,1)}) %all-gather.8.cloned.1.call-update) | async-done | bytes 8388624 | tf_op jit(solution)/shard_map/all_gather | solution.py:113
  256.4 40.4 %mlp.1 = (bf16[1536,1024]{1,0:T(8,128)(2,1)}, bf16[1536,1024]{1,0:T(8,128)(2,1)}, bf16[4,2,256,2048]{3,2,1,0:T(8,128)(2,1)}) custom-call(bf16[384,2048]{1,0:T(8,128)(2,1)} %copy-done.17, bf16[384,2048]{1,0:T(8,128)(2,1)} %collective-permute-done.13.refs_1_, bf16[384,2048]{1,0:T(8,128)(2,1)} %collective-permute-done.14.refs_2_, ...), custom_call_target="tpu_custom_call" | custom-call | flops 25769803776 | bytes 35651584 | tf_op jit(solution)/shard_map/mlp/pallas_call | solution.py:201
  296.8 7.8 %fusion.6 = bf16[768,2048]{1,0:T(8,128)(2,1)} fusion(bf16[2048,2048]{1,0:T(8,128)(2,1)} %all-gather.8.cloned.1.call-done, bf16[1536,1024]{1,0:T(8,128)(2,1)} %get-tuple-element.35), kind=kOutput, calls=%fused_computation.10 | convolution fusion | flops 3222798336 | bytes 8912896 | tf_op jit(solution)/shard_map/dot_general | solution.py:32
  310.6 7.1 %convert_add_fusion.2 = f32[768,2048]{1,0:T(8,128)S(1)} fusion(bf16[768,2048]{1,0:T(8,128)(2,1)} %collective-permute-done.16, bf16[2048,2048]{1,0:T(8,128)(2,1)} %all-gather.8.cloned.1.call-done, bf16[1536,1024]{1,0:T(8,128)(2,1)} %get-tuple-element.35), kind=kOutput, calls=%fused_computation.2 | convolution fusion | flops 3224371200 | bytes 15204352 | tf_op jit(solution)/shard_map/dot_general | solution.py:32
  319.4 18.9 %collective-permute-done.17 = bf16[384,2048]{1,0:T(8,128)(2,1)S(1)} collective-permute-done((bf16[384,2048]{1,0:T(8,128)(2,1)S(1)}, bf16[384,2048]{1,0:T(8,128)(2,1)S(1)}, u32[]{:S(2)}, u32[]{:S(2)}) %collective-permute-start.17) | collective-permute-done | bytes 1572896 | tf_op jit(solution)/shard_map/ppermute | solution.py:64
  340.7 10.5 %collective-permute-done.18 = bf16[192,2048]{1,0:T(8,128)(2,1)S(1)} collective-permute-done((bf16[192,2048]{1,0:T(8,128)(2,1)S(1)}, bf16[192,2048]{1,0:T(8,128)(2,1)S(1)}, u32[]{:S(2)}, u32[]{:S(2)}) %collective-permute-start.18) | collective-permute-done | bytes 786464 | tf_op jit(solution)/shard_map/ppermute | solution.py:60
  355.2 10.5 %collective-permute-done.19 = bf16[192,2048]{1,0:T(8,128)(2,1)S(1)} collective-permute-done((bf16[192,2048]{1,0:T(8,128)(2,1)S(1)}, bf16[192,2048]{1,0:T(8,128)(2,1)S(1)}, u32[]{:S(2)}, u32[]{:S(2)}) %collective-permute-start.19) | collective-permute-done | bytes 786464 | tf_op jit(solution)/shard_map/ppermute | solution.py:60
  367.5 18.9 %collective-permute-done.20 = bf16[384,2048]{1,0:T(8,128)(2,1)S(1)} collective-permute-done((bf16[384,2048]{1,0:T(8,128)(2,1)S(1)}, bf16[384,2048]{1,0:T(8,128)(2,1)S(1)}, u32[]{:S(2)}, u32[]{:S(2)}) %collective-permute-start.20) | collective-permute-done | bytes 1572896 | tf_op jit(solution)/shard_map/ppermute | solution.py:64
  395.9 12.5 %attend_back.1 = bf16[1536,768]{1,0:T(8,128)(2,1)} custom-call(s32[8]{0:T(128)} %convert_add_fusion.5.item_lengths, bf16[1536,768]{1,0:T(8,128)(2,1)} %convolution_convert_fusion.3.qkv, bf16[1536,256]{1,0:T(8,128)(2,1)} %convolution_convert_fusion.6.grad_mixed), custom_call_target="tpu_custom_call" | custom-call | flops 905969664 | bytes 5505024 | tf_op jit(solution)/shard_map/attend_back/pallas_call | solution.py:238
  408.5 9.1 %convolution_convert_fusion.4 = bf16[2048,768]{0,1:T(8,128)(2,1)} fusion(bf16[1536,2048]{1,0:T(8,128)(2,1)} %constant_dynamic-update-slice_fusion, bf16[1536,768]{1,0:T(8,128)(2,1)} %attend_back.1), kind=kOutput, calls=%fused_computation.15 | convolution fusion | flops 4833411072 | bytes 11796480 | tf_op jit(solution)/shard_map/dot_general | solution.py:26
  425.7 6.6 %convolution_convert_fusion.1 = bf16[768,2048]{1,0:T(8,128)(2,1)} fusion(bf16[2048,768]{1,0:T(8,128)(2,1)} %all-gather.4.cloned.1.call-done, bf16[1536,768]{1,0:T(8,128)(2,1)} %attend_back.1), kind=kOutput, calls=%fused_computation.12 | convolution fusion | flops 2417491968 | bytes 7471104 | tf_op jit(solution)/shard_map/dot_general | solution.py:32
  448.7 18.9 %collective-permute-done.28 = bf16[384,2048]{1,0:T(8,128)(2,1)S(1)} collective-permute-done((bf16[384,2048]{1,0:T(8,128)(2,1)S(1)}, bf16[384,2048]{1,0:T(8,128)(2,1)S(1)}, u32[]{:S(2)}, u32[]{:S(2)}) %collective-permute-start.28) | collective-permute-done | bytes 1572896 | tf_op jit(solution)/shard_map/ppermute | solution.py:64
  495.1 5.7 %all-to-all-done.3 = f32[32,1,128]{2,1,0:T(1,128)S(1)} async-done(((f32[32,1,128]{2,1,0:T(1,128)}), f32[32,1,128]{2,1,0:T(1,128)S(1)}, u32[]{:S(2)}, u32[]{:S(2)}) %all-to-all-start.3) | async-done | bytes 16416 | tf_op jit(solution)/shard_map/all_to_all | solution.py:377
  541.8 7.6 %all-to-all-done.4 = bf16[8,64,768]{2,1,0:T(8,128)(2,1)S(1)} async-done(((bf16[8,64,768]{2,1,0:T(8,128)(2,1)}), bf16[8,64,768]{2,1,0:T(8,128)(2,1)S(1)}, u32[]{:S(2)}, u32[]{:S(2)}) %all-to-all-start.4) | async-done | bytes 786464 | tf_op jit(solution)/shard_map/all_to_all | solution.py:391
  (260 shorter events, 206.0 us)
Async XLA Ops:
  7.2 87.8 %all-gather.6.cloned.1.call-start = ((), (), s32[]{:S(2)}) async-start(), calls=%async_computation.9 | async-start | bytes 1310720 | tf_op jit(solution)/shard_map/all_gather | solution.py:113
  19.6 24.3 %collective-permute-start.4 = (bf16[192,2048]{1,0:T(8,128)(2,1)S(1)}, bf16[192,2048]{1,0:T(8,128)(2,1)S(1)}, u32[]{:S(2)}, u32[]{:S(2)}) collective-permute-start(bf16[192,2048]{1,0:T(8,128)(2,1)S(1)} %get-tuple-element.52), channel_id=1, source_target_pairs={{0,2},{1,5},{2,0},{3,7},{4,6},{5,1},{6,4},{7,3},{8,10},{9,13},{10,... | collective-permute-start | bytes 2359304 | tf_op jit(solution)/shard_map/ppermute | solution.py:60
  35.1 80.5 %all-gather.4.cloned.1.call-start = ((), (), s32[]{:S(2)}) async-start(), calls=%async_computation.8 | async-start | bytes 3932160 | tf_op jit(solution)/shard_map/all_gather | solution.py:113
  43.4 19.5 %collective-permute-start = (bf16[192,2048]{1,0:T(8,128)(2,1)S(1)}, bf16[192,2048]{1,0:T(8,128)(2,1)S(1)}, u32[]{:S(2)}, u32[]{:S(2)}) collective-permute-start(bf16[192,2048]{1,0:T(8,128)(2,1)S(1)} %fusion.17), channel_id=1, source_target_pairs={{0,2},{1,5},{2,0},{3,7},{4,6},{5,1},{6,4},{7,3},{8,10},{9,13},{10,... | collective-permute-start | bytes 2359304 | tf_op jit(solution)/shard_map/ppermute | solution.py:60
  45.2 28.4 %collective-permute-start.5 = (bf16[384,2048]{1,0:T(8,128)(2,1)}, bf16[384,2048]{1,0:T(8,128)(2,1)}, u32[]{:S(2)}, u32[]{:S(2)}) collective-permute-start(bf16[384,2048]{1,0:T(8,128)(2,1)} %pad_maximum_fusion.4), channel_id=1, source_target_pairs={{0,4},{1,3},{2,6},{3,1},{4,0},{5,7},{6,2},{7,5},{8,12},{9,11},{10,... | collective-permute-start | bytes 4718600 | tf_op jit(solution)/shard_map/ppermute | solution.py:64
  63.0 31.1 %collective-permute-start.1 = (bf16[384,2048]{1,0:T(8,128)(2,1)S(1)}, bf16[384,2048]{1,0:T(8,128)(2,1)}, u32[]{:S(2)}, u32[]{:S(2)}) collective-permute-start(bf16[384,2048]{1,0:T(8,128)(2,1)S(1)} %pad_maximum_fusion.3), channel_id=1, source_target_pairs={{0,4},{1,3},{2,6},{3,1},{4,0},{5,7},{6,2},{7,5},{8,12},{9,11},{10,... | collective-permute-start | bytes 4718600 | tf_op jit(solution)/shard_map/ppermute | solution.py:64
  65.3 35.3 %all-to-all-start.1 = ((bf16[8,64,1024]{2,1,0:T(8,128)(2,1)}), bf16[8,64,1024]{2,1,0:T(8,128)(2,1)}, u32[]{:S(2)}, u32[]{:S(2)}) async-start(bf16[8,64,1024]{2,1,0:T(8,128)(2,1)} %reshape.227), calls=%async_computation.1 | async-start | bytes 2097152 | tf_op jit(solution)/shard_map/all_to_all | solution.py:285
  69.5 186.8 %all-gather.8.cloned.1.call-start = ((), (), s32[]{:S(2)}) async-start(), calls=%async_computation.10 | async-start | bytes 10485760 | tf_op jit(solution)/shard_map/all_gather | solution.py:113
  73.0 32.6 %collective-permute-start.6 = (bf16[384,2048]{1,0:T(8,128)(2,1)}, bf16[384,2048]{1,0:T(8,128)(2,1)}, u32[]{:S(2)}, u32[]{:S(2)}) collective-permute-start(bf16[384,2048]{1,0:T(8,128)(2,1)} %pad_maximum_fusion.4), channel_id=1, source_target_pairs={{0,1},{1,0},{2,3},{3,2},{4,5},{5,4},{6,7},{7,6},{8,9},{9,8},{10,11... | collective-permute-start | bytes 4718600 | tf_op jit(solution)/shard_map/ppermute | solution.py:68
  73.4 32.2 %collective-permute-start.2 = (bf16[384,2048]{1,0:T(8,128)(2,1)S(1)}, bf16[384,2048]{1,0:T(8,128)(2,1)}, u32[]{:S(2)}, u32[]{:S(2)}) collective-permute-start(bf16[384,2048]{1,0:T(8,128)(2,1)S(1)} %pad_maximum_fusion.3), channel_id=1, source_target_pairs={{0,1},{1,0},{2,3},{3,2},{4,5},{5,4},{6,7},{7,6},{8,9},{9,8},{10,11... | collective-permute-start | bytes 4718600 | tf_op jit(solution)/shard_map/ppermute | solution.py:68
  73.6 32.0 %collective-permute-start.7 = (bf16[384,2048]{1,0:T(8,128)(2,1)}, bf16[384,2048]{1,0:T(8,128)(2,1)}, u32[]{:S(2)}, u32[]{:S(2)}) collective-permute-start(bf16[384,2048]{1,0:T(8,128)(2,1)} %collective-permute-done.5), channel_id=1, source_target_pairs={{0,1},{1,0},{2,3},{3,2},{4,5},{5,4},{6,7},{7,6},{8,9},{9,8},{10,11... | collective-permute-start | bytes 4718600 | tf_op jit(solution)/shard_map/ppermute | solution.py:68
  103.4 398.8 %reduce-scatter.5.cloned.1.call-start = ((), (), s32[]{:S(2)}) async-start(), calls=%async_computation.12 | async-start | bytes 10485760 | tf_op jit(solution)/shard_map/reduce_scatter | solution.py:117
  143.9 20.5 %collective-permute-start.10 = (bf16[384,2048]{1,0:T(8,128)(2,1)S(1)}, bf16[384,2048]{1,0:T(8,128)(2,1)S(1)}, u32[]{:S(2)}, u32[]{:S(2)}) collective-permute-start(bf16[384,2048]{1,0:T(8,128)(2,1)S(1)} %slice.327), channel_id=1, source_target_pairs={{0,4},{1,3},{2,6},{3,1},{4,0},{5,7},{6,2},{7,5},{8,12},{9,11},{10,... | collective-permute-start | bytes 4718600 | tf_op jit(solution)/shard_map/ppermute | solution.py:64
  193.8 20.6 %collective-permute-start.13 = (bf16[384,2048]{1,0:T(8,128)(2,1)S(1)}, bf16[384,2048]{1,0:T(8,128)(2,1)}, u32[]{:S(2)}, u32[]{:S(2)}) collective-permute-start(bf16[384,2048]{1,0:T(8,128)(2,1)S(1)} %pad_maximum_fusion.5.refs_0_), channel_id=1, source_target_pairs={{0,4},{1,3},{2,6},{3,1},{4,0},{5,7},{6,2},{7,5},{8,12},{9,11},{10,... | collective-permute-start | bytes 4718600 | tf_op jit(solution)/shard_map/ppermute | solution.py:64
  195.3 28.3 %collective-permute-start.14 = (bf16[384,2048]{1,0:T(8,128)(2,1)S(1)}, bf16[384,2048]{1,0:T(8,128)(2,1)}, u32[]{:S(2)}, u32[]{:S(2)}) collective-permute-start(bf16[384,2048]{1,0:T(8,128)(2,1)S(1)} %pad_maximum_fusion.5.refs_0_), channel_id=1, source_target_pairs={{0,1},{1,0},{2,3},{3,2},{4,5},{5,4},{6,7},{7,6},{8,9},{9,8},{10,11... | collective-permute-start | bytes 4718600 | tf_op jit(solution)/shard_map/ppermute | solution.py:68
  214.4 42.0 %collective-permute-start.15 = (bf16[384,2048]{1,0:T(8,128)(2,1)}, bf16[384,2048]{1,0:T(8,128)(2,1)}, u32[]{:S(2)}, u32[]{:S(2)}) collective-permute-start(bf16[384,2048]{1,0:T(8,128)(2,1)} %collective-permute-done.13.refs_1_), channel_id=1, source_target_pairs={{0,1},{1,0},{2,3},{3,2},{4,5},{5,4},{6,7},{7,6},{8,9},{9,8},{10,11... | collective-permute-start | bytes 4718600 | tf_op jit(solution)/shard_map/ppermute | solution.py:68
  304.6 226.1 %reduce-scatter.3.cloned.1.call-start = ((), (), s32[]{:S(2)}) async-start(), calls=%async_computation.11 | async-start | bytes 5242880 | tf_op jit(solution)/shard_map/reduce_scatter | solution.py:117
  317.9 20.5 %collective-permute-start.17 = (bf16[384,2048]{1,0:T(8,128)(2,1)S(1)}, bf16[384,2048]{1,0:T(8,128)(2,1)S(1)}, u32[]{:S(2)}, u32[]{:S(2)}) collective-permute-start(bf16[384,2048]{1,0:T(8,128)(2,1)S(1)} %slice.326), channel_id=1, source_target_pairs={{0,4},{1,3},{2,6},{3,1},{4,0},{5,7},{6,2},{7,5},{8,12},{9,11},{10,... | collective-permute-start | bytes 4718600 | tf_op jit(solution)/shard_map/ppermute | solution.py:64
  365.9 20.5 %collective-permute-start.20 = (bf16[384,2048]{1,0:T(8,128)(2,1)S(1)}, bf16[384,2048]{1,0:T(8,128)(2,1)S(1)}, u32[]{:S(2)}, u32[]{:S(2)}) collective-permute-start(bf16[384,2048]{1,0:T(8,128)(2,1)S(1)} %pad_maximum_fusion.6), channel_id=1, source_target_pairs={{0,4},{1,3},{2,6},{3,1},{4,0},{5,7},{6,2},{7,5},{8,12},{9,11},{10,... | collective-permute-start | bytes 4718600 | tf_op jit(solution)/shard_map/ppermute | solution.py:64
  392.7 24.9 %collective-permute-start.23 = (bf16[2,64,2048]{2,1,0:T(8,128)(2,1)}, bf16[2,64,2048]{2,1,0:T(8,128)(2,1)}, u32[]{:S(2)}, u32[]{:S(2)}) collective-permute-start(bf16[2,64,2048]{2,1,0:T(8,128)(2,1)} %select_bitcast_fusion), channel_id=1, source_target_pairs={{0,1},{1,0},{2,3},{3,2},{4,5},{5,4},{6,7},{7,6},{8,9},{9,8},{10,11... | collective-permute-start | bytes 1572872 | tf_op jit(solution)/shard_map/ppermute | solution.py:68
  442.1 30.0 %collective-permute-start.25 = (bf16[768,2048]{1,0:T(8,128)(2,1)S(1)}, bf16[768,2048]{1,0:T(8,128)(2,1)S(1)}, u32[]{:S(2)}, u32[]{:S(2)}) collective-permute-start(bf16[768,2048]{1,0:T(8,128)(2,1)S(1)} %convolution_convert_fusion), channel_id=1, source_target_pairs={{0,1},{1,0},{2,3},{3,2},{4,5},{5,4},{6,7},{7,6},{8,9},{9,8},{10,11... | collective-permute-start | bytes 9437192 | tf_op jit(solution)/shard_map/ppermute | solution.py:68
  447.1 20.5 %collective-permute-start.28 = (bf16[384,2048]{1,0:T(8,128)(2,1)S(1)}, bf16[384,2048]{1,0:T(8,128)(2,1)S(1)}, u32[]{:S(2)}, u32[]{:S(2)}) collective-permute-start(bf16[384,2048]{1,0:T(8,128)(2,1)S(1)} %slice.324), channel_id=1, source_target_pairs={{0,4},{1,3},{2,6},{3,1},{4,0},{5,7},{6,2},{7,5},{8,12},{9,11},{10,... | collective-permute-start | bytes 4718600 | tf_op jit(solution)/shard_map/ppermute | solution.py:64
  479.7 28.4 %collective-permute-start.26 = (bf16[384,2048]{1,0:T(8,128)(2,1)}, bf16[384,2048]{1,0:T(8,128)(2,1)}, u32[]{:S(2)}, u32[]{:S(2)}) collective-permute-start(bf16[384,2048]{1,0:T(8,128)(2,1)} %slice.325), channel_id=1, source_target_pairs={{0,4},{1,3},{2,6},{3,1},{4,0},{5,7},{6,2},{7,5},{8,12},{9,11},{10,... | collective-permute-start | bytes 4718600 | tf_op jit(solution)/shard_map/ppermute | solution.py:64
  513.7 25.2 %collective-permute-start.27 = (bf16[192,2048]{1,0:T(8,128)(2,1)}, bf16[192,2048]{1,0:T(8,128)(2,1)}, u32[]{:S(2)}, u32[]{:S(2)}) collective-permute-start(bf16[192,2048]{1,0:T(8,128)(2,1)} %slice.329), channel_id=1, source_target_pairs={{0,2},{1,5},{2,0},{3,7},{4,6},{5,1},{6,4},{7,3},{8,10},{9,13},{10,... | collective-permute-start | bytes 2359304 | tf_op jit(solution)/shard_map/ppermute | solution.py:60
  (49 other events, 515.5 us)
Sparse Core Ops, SparseCore 0:
  9.6 31.5 all-gather.5
  43.3 62.6 all-gather.3
  108.1 148.2 all-gather.7
  304.7 142.9 reduce-scatter.4
  449.9 77.6 reduce-scatter.2
